TPU v7x, 256 devices: a whole 4x4x8 slice. The times are simulated.
256 devices in a mesh: seq: 2 (over z_lo), shard: 128 (over x, z_hi, y, core).
Axes of the slice: x: 4, y: 4, z: 8 (z_hi: 4, z_lo: 2; z = z_hi * 2 + z_lo), core: 2. Of those that a mesh axis runs over, the one named last changes fastest.
Arguments:
- tokens: bfloat16 [65536, 768], P(('shard', 'seq')), may hold values from -24 to 24
- w_qkv: bfloat16 [768, 2304], P('shard'), may hold values from -0.3125 to 0.3125
- bias_q: bfloat16 [768], P('shard'), may hold values from -1.1953125 to 1.1953125
- bias_v: bfloat16 [768], P('shard'), may hold values from -1.1953125 to 1.1953125
- w_out: bfloat16 [768, 768], P('shard'), may hold values from -0.4375 to 0.4375
- bias_out: bfloat16 [768], P('shard'), may hold values from -1.1953125 to 1.1953125
- gain_one: bfloat16 [768], P('shard'), may hold values from 0.5 to 1.5
- shift_one: bfloat16 [768], P('shard'), may hold values from -1.1953125 to 1.1953125
- w_in: bfloat16 [768, 3072], P('shard'), may hold values from -0.21875 to 0.21875
- bias_in: bfloat16 [3072], P('shard'), may hold values from -1.1953125 to 1.1953125
- w_down: bfloat16 [3072, 768], P('shard'), may hold values from -0.15625 to 0.15625
- bias_down: bfloat16 [768], P('shard'), may hold values from -1.1953125 to 1.1953125
- gain_two: bfloat16 [768], P('shard'), may hold values from 0.5 to 1.5
- shift_two: bfloat16 [768], P('shard'), may hold values from -1.1953125 to 1.1953125
- doc_lengths: int32 [128], replicated, may hold values from 1 to 1024, 65536 in all
- cotangent: bfloat16 [65536, 768], P(('shard', 'seq')), may hold values from -6 to 6
Outputs:
- layer_out: bfloat16 [65536, 768], P(('shard', 'seq'))
- grad_tokens: float32 [65536, 768], P(('shard', 'seq'))
- grad_w_qkv: float32 [768, 2304], P('shard')
- grad_bias_q: float32 [768], P('shard')
- grad_bias_v: float32 [768], P('shard')
- grad_w_out: float32 [768, 768], P('shard')
- grad_bias_out: float32 [768], P('shard')
- grad_gain_one: float32 [768], P('shard')
- grad_shift_one: float32 [768], P('shard')
- grad_w_in: float32 [768, 3072], P('shard')
- grad_bias_in: float32 [3072], P('shard')
- grad_w_down: float32 [3072, 768], P('shard')
- grad_bias_down: float32 [768], P('shard')
- grad_gain_two: float32 [768], P('shard')
- grad_shift_two: float32 [768], P('shard')
Inputs may be any that keep to these rules, and one draw needn't show every extreme that they name: `doc_lengths`: document lengths in stream order; the documents fill the 65536 tokens end to end, and the longest has exactly 1024 tokens.
All inputs are finite; a program needn't handle non-finite values.
Results may differ from a plain program's by a relative error of at most 0.025.
Values may be sent and summed in bfloat16 or wider, within the bound.
A program may use at most 192 MiB of HBM per device.

v0:
```python
import functools
import jax
import jax.numpy as jnp
from jax import lax
from jax.experimental import pallas as pl
from jax.experimental.pallas import tpu as pltpu
from jax.sharding import PartitionSpec as P

HEAD_DIM = 64
NORM_EPS = 1e-12
MESH = pl.DeviceIdType.MESH
ANY_SPACE = pl.BlockSpec(memory_space=pl.ANY)
IN_VMEM = pl.BlockSpec(memory_space=pltpu.VMEM)
LOG2E = 1.4426950408889634
TILE = 256
HALF = 384
BOTTOM = -1e30
EXTENT = {"x": 4, "y": 4, "z": 8}
ORDERS = (("z", "y", "x"), ("z", "y", "x"), ("z", "x", "y"))
OTHERS = {dim: range(1, size) for dim, size in EXTENT.items()}
HALVES = (((0, 256), (256, 128)), ((0, 128), (128, 256)), ((0, 256), (256, 128)))
STREAMS = (0, 1, 2)
WIDE = (2, 2, 4, 4, 2, 3, 8, HALF)
TALL = (4, 4, 2, 2, 2, 3, 8, HALF)


def place():
    s = lax.axis_index("shard")
    q = lax.axis_index("seq")
    return {
        "c": lax.rem(s, 2),
        "y": lax.rem(s // 2, 4),
        "x": s // 32,
        "z": lax.rem(s // 8, 4) * 2 + q,
    }


def device_at(at):
    return {
        "shard": ((at["x"] * 4 + at["z"] // 2) * 4 + at["y"]) * 2 + at["c"],
        "seq": lax.rem(at["z"], 2),
    }


def moved(at, **steps):
    new = dict(at)
    for dim, step in steps.items():
        size = 2 if dim == "c" else EXTENT[dim]
        new[dim] = lax.rem(at[dim] + step + size, size)
    return new


def stream_mates():
    s = lax.axis_index("shard")
    q = lax.axis_index("seq")
    partner = {"shard": s, "seq": 1 - q}
    after = {"shard": lax.rem(s + 2, 128), "seq": q}
    before = {"shard": lax.rem(s + 126, 128), "seq": q}
    return partner, before, after


def greet(targets):
    barrier = pltpu.get_barrier_semaphore()
    for target in targets:
        pl.semaphore_signal(barrier, inc=1, device_id=target, device_id_type=MESH)
    pl.semaphore_wait(barrier, len(targets))


def sending(src, dst, send, recv, target):
    return pltpu.make_async_remote_copy(
        src_ref=src, dst_ref=dst, send_sem=send, recv_sem=recv, device_id=target, device_id_type=MESH
    )


def neighbours(at):
    return [moved(at, **{d: step}) for d in ("x", "y", "z") for step in (1, -1)]


def octet_mates(me):
    across = dict(me)
    across["y"] = me["y"] + 1 - 2 * lax.rem(me["y"], 2)
    twin = moved(me, c=1)
    diagonal = dict(across)
    diagonal["c"] = twin["c"]
    return twin, across, diagonal


def span(index):
    return slice(None) if index is None else pl.ds(index, 1)


def picks_of(sets, gone=()):
    x, y, z = sets["x"], sets["y"], sets["z"]
    pick = {
        "x": x,
        "m": None if y is None else y // 2,
        "yp": None if y is None else lax.rem(y, 2),
        "zh": None if z is None else z // 2,
        "q": None if z is None else lax.rem(z, 2),
    }
    names = {"x": ("x",), "y": ("m", "yp"), "z": ("zh", "q")}
    for dim in gone:
        for name in names[dim]:
            pick[name] = 0
    return pick


WIDE_DIMS = ("yp", "q", "x", "zh", "m")
TALL_DIMS = ("x", "zh", "m", "yp", "q")
DIM_SIZE = {"yp": 2, "q": 2, "x": 4, "zh": 4, "m": 2}


def dims_of(k):
    return TALL_DIMS if k == 2 else WIDE_DIMS


def view(ref, k, part, sets, half=None, gone=(), lead=()):
    pick = picks_of(sets, gone)
    cut = (0, HALF) if half is None else HALVES[k][half]
    at = tuple(span(pick[d]) for d in dims_of(k))
    rows = () if part is None else (part,)
    return ref.at[(*lead, *at, *rows, slice(None), pl.ds(*cut))]


def gather_kernel(
    cat_ref, down_ref, vec_ref, tok_ref, first, second, third, vecs, window,
    land, stage, own, oct_s, oct_r, local, near_s, near_r, send, recv, core_s, core_r, vec_s, vec_r, tok_s, tok_r,
):
    me = place()
    c, x, y, z = me["c"], me["x"], me["y"], me["z"]
    yp, q, m, zh = lax.rem(y, 2), lax.rem(z, 2), y // 2, z // 2
    outs = (first, second, third)
    twin, across, diagonal = octet_mates(me)
    twin_id = device_at(twin)
    partner, before, after = stream_mates()
    lines = [moved(me, **{d: o}) for d in EXTENT for o in OTHERS[d]]
    greet([device_at(a) for a in lines + [twin, diagonal]] + [before, after])

    def chunk_of(at):
        cols = (lax.rem(at["y"], 2) * 2 + q) * 768 + at["c"] * HALF
        return cat_ref.at[:, :, pl.ds(pl.multiple_of(cols, 128), HALF)]

    index = yp * 2 + c
    mates = (twin, across, diagonal)
    out = [
        sending(chunk_of(mate), land.at[:, index], oct_s.at[k], oct_r.at[k], device_at(mate))
        for k, mate in enumerate(mates)
    ]
    for cp in out:
        cp.start()
    kept = pltpu.make_async_copy(chunk_of(me), land.at[:, index], local.at[0])
    kept.start()
    gives = q == c
    down_out = sending(
        down_ref.at[:, :, pl.ds(pl.multiple_of((1 - c) * HALF, 128), HALF)], own.at[2], oct_s.at[3], oct_r.at[3], twin_id
    )
    down_kept = pltpu.make_async_copy(
        down_ref.at[:, :, pl.ds(pl.multiple_of(c * HALF, 128), HALF)], own.at[2], local.at[1]
    )

    @pl.when(gives)
    def _():
        down_out.start()
        down_kept.start()

    vec_kept = pltpu.make_async_copy(vec_ref, vecs.at[c, x, zh, y], local.at[2])
    vec_kept.start()

    sent = []

    def go(src, dst, send_sem, recv_sem, target):
        cp = sending(src, dst, send_sem, recv_sem, target)
        cp.start()
        sent.append(cp)

    def arrive(dst, send_sem, recv_sem, target):
        sending(dst, dst, send_sem, recv_sem, target).wait_recv()

    def tok_go(src, dst, at, target):
        go(src, dst, tok_s.at[at], tok_r.at[at], target)

    tok_kept = pltpu.make_async_copy(tok_ref, window.at[1, c, q], local.at[3])
    tok_kept.start()
    tok_go(tok_ref, window.at[1, c, q], 0, partner)
    tok_go(tok_ref, window.at[0, c, q], 1, after)
    tok_go(tok_ref, window.at[2, c, q], 2, before)
    tok_go(tok_ref, window.at[1, c, q], 3, twin_id)

    def tok_forward():
        theirs = window.at[1, c, 1 - q]
        arrive(theirs, tok_s.at[0], tok_r.at[0], partner)
        tok_go(theirs, window.at[0, c, 1 - q], 4, after)
        tok_go(theirs, window.at[2, c, 1 - q], 5, before)
        tok_go(theirs, window.at[1, c, 1 - q], 6, twin_id)

    def tok_share(h, first_slot, at):
        arrive(window.at[0, c, h], tok_s.at[first_slot], tok_r.at[first_slot], before)
        arrive(window.at[2, c, h], tok_s.at[first_slot + 1], tok_r.at[first_slot + 1], after)
        tok_go(window.at[0, c, h], window.at[0, c, h], at, twin_id)
        tok_go(window.at[2, c, h], window.at[2, c, h], at + 1, twin_id)

    vec_rounds = (("x", (1, 2, 3)), ("y", (1, 2, 3)), ("z", (2, 4, 6)), ("c", (1,)))

    def vec_copies(number, arriving):
        dim, steps = vec_rounds[number]
        done = [d for d, _ in vec_rounds[:number]]
        copies = []
        for k, step in enumerate(steps):
            source = moved(me, **{dim: (1 if dim == "c" else -step)}) if arriving else me
            pick = [None if d in done else (source["z"] // 2 if d == "z" else source[d]) for d in ("c", "x", "z", "y")]
            ref = vecs.at[tuple(span(p) for p in pick)]
            copies.append(
                sending(ref, ref, vec_s.at[number, k], vec_r.at[number, k], device_at(moved(me, **{dim: step})))
            )
        return copies

    def vec_start(number):
        for cp in vec_copies(number, False):
            cp.start()
            sent.append(cp)

    def vec_wait(number):
        for cp in vec_copies(number, True):
            cp.wait_recv()

    kept.wait()
    for k, mate in enumerate(mates):
        mate_index = lax.rem(mate["y"], 2) * 2 + mate["c"]
        arrive(land.at[:, mate_index], oct_s.at[k], oct_r.at[k], device_at(mate))
    for k in range(2):
        for owner in range(4):
            stage[pl.ds(6 * owner, 6), :] = land[k, owner].astype(jnp.float32)
        for part in range(3):
            own[k, part] = stage[pl.ds(8 * part, 8), :].astype(jnp.bfloat16)

    @pl.when(gives)
    def _():
        down_kept.wait()

    @pl.when(jnp.logical_not(gives))
    def _():
        down_out.wait_recv()

    homes = (first.at[c, yp, q, x, zh, m], second.at[c, yp, q, x, zh, m], third.at[c, x, zh, m, yp, q])
    flush = [pltpu.make_async_copy(own.at[k], homes[k], local.at[4 + k]) for k in STREAMS]
    for cp in flush:
        cp.start()
    twins = []

    def share(k, part, sets, half, slot):
        mine = view(outs[k], k, part, sets, half, (), (c,))
        theirs = view(outs[k], k, part, sets, half, (), (1 - c,))
        go(mine, mine, core_s.at[slot, k], core_r.at[slot, k], twin_id)
        twins.append((theirs, core_s.at[slot, k], core_r.at[slot, k]))

    def sets_at(part, phase, index):
        sets = {"x": x, "y": y, "z": z}
        for earlier in ORDERS[part][:phase]:
            sets[earlier] = None
        dim = ORDERS[part][phase]
        sets[dim] = lax.rem(index + EXTENT[dim], EXTENT[dim])
        return sets

    def near(k, part, phase, arriving):
        dim = ORDERS[part][phase]
        for o in OTHERS[dim]:
            sems = near_s.at[part, phase, o, k], near_r.at[part, phase, o, k]
            target = device_at(moved(me, **{dim: o}))
            if arriving:
                arrive(view(outs[k], k, part, sets_at(part, phase, me[dim] - o), None, (), (c,)), *sems, target)
            elif phase == 0:
                go(own.at[k, part], homes[k].at[part], *sems, target)
            else:
                ref = view(outs[k], k, part, sets_at(part, phase, me[dim]), None, (), (c,))
                go(ref, ref, *sems, target)

    def ring(k, part, step, arriving):
        dim = ORDERS[part][2]
        size = EXTENT[dim]
        for direction, sign in enumerate((1, -1)):
            sets = sets_at(part, 2, me[dim] - sign * (step if arriving else step - 1))
            half = direction if step == size // 2 else None
            ref = view(outs[k], k, part, sets, half, (), (c,))
            slot = part * 2 + step - 1
            sems = send.at[slot, direction, k], recv.at[slot, direction, k]
            target = device_at(moved(me, **{dim: sign}))
            if arriving:
                arrive(ref, *sems, target)
            else:
                go(ref, ref, *sems, target)

    def ring_share(k, part, step):
        dim = ORDERS[part][2]
        for direction, sign in enumerate((1, -1)):
            half = direction if step == EXTENT[dim] // 2 else None
            share(k, part, sets_at(part, 2, me[dim] - sign * step), half, 3 + (part * 2 + step - 1) * 2 + direction)

    for k in STREAMS:
        for part in range(3):
            near(k, part, 0, False)
    vec_kept.wait()
    vec_start(0)
    for cp in flush:
        cp.wait()
    for k in STREAMS:
        for part in range(3):
            near(k, part, 0, True)
            near(k, part, 1, False)
    tok_forward()
    vec_wait(0)
    vec_start(1)
    for k in STREAMS:
        for part in range(3):
            near(k, part, 1, True)
            ring(k, part, 1, False)
    for k in STREAMS:
        for part in range(3):
            share(k, part, sets_at(part, 2, me[ORDERS[part][2]]), None, part)
    vec_wait(1)
    vec_start(2)
    for k in STREAMS:
        for part in range(3):
            ring(k, part, 1, True)
            ring(k, part, 2, False)
            ring_share(k, part, 1)
    vec_wait(2)
    vec_start(3)
    tok_share(q, 1, 7)
    for k in STREAMS:
        for part in range(3):
            ring(k, part, 2, True)
            ring_share(k, part, 2)
    tok_share(1 - q, 4, 9)
    vec_wait(3)
    for ref, send_sem, recv_sem in twins:
        arrive(ref, send_sem, recv_sem, twin_id)
    arrive(window.at[1, 1 - c, q], tok_s.at[3], tok_r.at[3], twin_id)
    arrive(window.at[1, 1 - c, 1 - q], tok_s.at[6], tok_r.at[6], twin_id)
    for h, at in ((q, 7), (1 - q, 9)):
        arrive(window.at[0, 1 - c, h], tok_s.at[at], tok_r.at[at], twin_id)
        arrive(window.at[2, 1 - c, h], tok_s.at[at + 1], tok_r.at[at + 1], twin_id)
    tok_kept.wait()
    for cp in out + sent:
        cp.wait_send()

    @pl.when(gives)
    def _():
        down_out.wait_send()


def gather(cat, down, vec, tokens):
    dma = pltpu.SemaphoreType.DMA
    return pl.pallas_call(
        gather_kernel,
        name="gather",
        out_shape=(
            jax.ShapeDtypeStruct((2, *WIDE), jnp.bfloat16),
            jax.ShapeDtypeStruct((2, *WIDE), jnp.bfloat16),
            jax.ShapeDtypeStruct((2, *TALL), jnp.bfloat16),
            jax.ShapeDtypeStruct((2, 4, 4, 4, 8, 128), jnp.float32),
            jax.ShapeDtypeStruct((3, 2, 2, TILE, 768), jnp.bfloat16),
        ),
        in_specs=[ANY_SPACE] * 4,
        out_specs=(ANY_SPACE,) * 5,
        scratch_shapes=[
            pltpu.VMEM((2, 4, 6, HALF), jnp.bfloat16),
            pltpu.VMEM((24, HALF), jnp.float32),
            pltpu.VMEM((3, 3, 8, HALF), jnp.bfloat16),
            dma((4,)), dma((4,)), dma((7,)), dma((3, 2, 8, 3)), dma((3, 2, 8, 3)), dma((6, 2, 3)), dma((6, 2, 3)),
            dma((15, 3)), dma((15, 3)),
            dma((4, 3)), dma((4, 3)), dma((11,)), dma((11,)),
        ],
        compiler_params=pltpu.CompilerParams(collective_id=1, has_side_effects=True, vmem_limit_bytes=58 << 20),
    )(cat, down, vec, tokens)


def reduce_kernel(*refs):
    (g0, g0_other, g1, g2, gv, dx, base, out0, out1, out2, out_v, out_tok) = refs[:12]
    grads = (None, g1, g2)
    refs = refs[12:]
    acc, other, refs = refs[:3], refs[3:6], refs[6:]
    lands = {}
    for n, (part, phase, k) in enumerate((a, b, k) for a in range(3) for b in range(3) for k in STREAMS):
        lands[part, phase, k] = refs[n]
    refs = refs[27:]
    (
        stage, rows, tall_f, v_c, v_x, v_y, v_z, t_acc, t_in, t_land, t_part, t_mate, t_base, t_out,
        local, core_s, core_r, near_s, near_r, send, recv, fin_s, fin_r, t_s, t_r, vec_s, vec_r, tok_s, tok_r, tok_l,
    ) = refs
    me = place()
    c, x, y, z = me["c"], me["x"], me["y"], me["z"]
    yp, q, m, zh = lax.rem(y, 2), lax.rem(z, 2), y // 2, z // 2
    twin, across, diagonal = octet_mates(me)
    twin_id = device_at(twin)
    partner, before, after = stream_mates()

    def other_q(at):
        new = dict(at)
        new["z"] = at["z"] + 1 - 2 * lax.rem(at["z"], 2)
        return new

    ring_mates = [moved(me, **{d: k}) for d in ("x", "y", "z") for k in range(1, EXTENT[d])]
    mates = [twin, across, diagonal] + [other_q(a) for a in (me, twin, across, diagonal)]
    targets = ring_mates + [twin, diagonal] + [other_q(a) for a in (twin, across, diagonal)]
    greet([device_at(a) for a in targets] + [before, after])
    sent = []

    def go(src, dst, send_sem, recv_sem, target):
        cp = sending(src, dst, send_sem, recv_sem, target)
        cp.start()
        sent.append(cp)

    def arrive(dst, send_sem, recv_sem, target):
        sending(dst, dst, send_sem, recv_sem, target).wait_recv()

    def order_of(part):
        return ORDERS[part][::-1]

    def sets_of(part, phase, index):
        sets = {"x": x, "y": y, "z": z}
        order = order_of(part)
        for later in order[phase + 1:]:
            sets[later] = None
        sets[order[phase]] = lax.rem(index + 2 * EXTENT[order[phase]], EXTENT[order[phase]])
        return sets

    def add_region(k, part, sets, sources, half=None, gone=()):
        pick, from_pick = picks_of(sets), picks_of(sets, gone)
        dims = dims_of(k)
        inner = dims[3:] if k < 2 else dims[2:]
        outer = [d for d in dims if d not in inner and pick[d] is None]
        count = 1
        for d in outer:
            count *= DIM_SIZE[d]
        cut = pl.ds(*((0, HALF) if half is None else HALVES[k][half]))

        def one(i):
            at = {}
            for d in reversed(outer):
                at[d] = lax.rem(i, DIM_SIZE[d]) if count > 1 else 0
                i = i // DIM_SIZE[d]

            def index(picked):
                return tuple(
                    (at[d] if d in at else slice(None)) if picked[d] is None else pl.ds(picked[d], 1) if d in inner else picked[d]
                    for d in dims
                )

            to = (*index(pick), part, slice(None), cut)
            fr = (*index(from_pick), slice(None), cut)
            if len(sources) == 1:
                acc[k][to] = acc[k][to] + sources[0][fr]
            else:
                total = acc[k][to].astype(jnp.float32)
                for src in sources:
                    total = total + src[fr].astype(jnp.float32)
                acc[k][to] = total.astype(jnp.bfloat16)

        if count == 1:
            one(0)
        else:
            lax.fori_loop(0, count, lambda i, carry: (one(i), carry)[1], 0)

    def hop(part, n):
        return sets_of(part, 0, me[order_of(part)[0]] + (2, 1, -1, 0)[n])

    own_copies = {}

    def cross(k, part, n):
        slot = part * 4 + n
        sets = hop(part, n)
        src = view(grads[k], k, part, sets, None, (), (1 - c,))
        go(src, view(other[k], k, part, sets), core_s.at[slot, k], core_r.at[slot, k], twin_id)
        kept = pltpu.make_async_copy(
            view(grads[k], k, part, sets, None, (), (c,)), view(acc[k], k, part, sets), local.at[slot, k]
        )
        kept.start()
        own_copies[k, part, n] = kept

    for part in range(3):
        go(g0_other.at[:, :, :, part], other[0].at[:, :, :, part], core_s.at[part, 0], core_r.at[part, 0], twin_id)
        whole = (slice(None),) * 5 + (part,)
        own_copies[0, part] = pltpu.make_async_copy(g0.at[whole], acc[0].at[whole], local.at[part, 0])
        own_copies[0, part].start()
    for n in range(4):
        for k in (1, 2):
            for part in range(3):
                cross(k, part, n)

    go(dx.at[:, 1 - c], t_in, tok_s.at[0], tok_r.at[0], twin_id)
    tok_kept = pltpu.make_async_copy(dx.at[:, c], t_acc, tok_l.at[0])
    tok_kept.start()
    base_kept = pltpu.make_async_copy(base, t_base, tok_l.at[1])
    base_kept.start()

    vec_lands = (v_c, v_x, v_y, v_z)
    vec_dims = ("c", "x", "y", "z")

    def vec_start(number):
        dim, land = vec_dims[number], vec_lands[number]
        for k in range(1, land.shape[0]):
            mine = land.at[me[dim]]
            go(mine, mine, vec_s.at[number, k], vec_r.at[number, k], device_at(moved(me, **{dim: k})))

    def vec_finish(number):
        dim, land = vec_dims[number], vec_lands[number]
        size = land.shape[0]
        for k in range(1, size):
            theirs = land.at[lax.rem(me[dim] - k + size, size)]
            arrive(theirs, vec_s.at[number, k], vec_r.at[number, k], device_at(moved(me, **{dim: k})))
        total = land[0]
        for k in range(1, size):
            total = total + land[k]
        return total

    def row_blocks(fn):
        lax.fori_loop(0, TILE // 32, lambda r, carry: (fn(pl.ds(pl.multiple_of(r * 32, 32), 32)), carry)[1], 0)

    def tok_cross():
        tok_kept.wait()
        arrive(t_in, tok_s.at[0], tok_r.at[0], twin_id)
        for n, h in enumerate((1 - q, q)):
            for r in (0, 2):
                def one(at):
                    t_acc[r, h, at] = t_acc[r, h, at] + t_in[r, h, at]
                row_blocks(one)
            go(t_acc.at[0, h], t_land.at[1, h], tok_s.at[1 + n], tok_r.at[1 + n], before)
            go(t_acc.at[2, h], t_land.at[0, h], tok_s.at[3 + n], tok_r.at[3 + n], after)

    def tok_total(h, at):
        f = jnp.float32
        return t_acc[1, h, at].astype(f) + t_in[1, h, at].astype(f) + t_land[0, h, at].astype(f) + t_land[1, h, at].astype(f)

    def tok_theirs():
        h = 1 - q
        arrive(t_land.at[1, h], tok_s.at[1], tok_r.at[1], after)
        arrive(t_land.at[0, h], tok_s.at[3], tok_r.at[3], before)

        def one(at):
            t_part[at] = tok_total(h, at).astype(jnp.bfloat16)
        row_blocks(one)
        go(t_part, t_mate, tok_s.at[5], tok_r.at[5], partner)

    def tok_mine():
        arrive(t_land.at[1, q], tok_s.at[2], tok_r.at[2], after)
        arrive(t_land.at[0, q], tok_s.at[4], tok_r.at[4], before)
        arrive(t_mate, tok_s.at[5], tok_r.at[5], partner)
        base_kept.wait()

        def one(at):
            t_out[at] = tok_total(q, at) + t_mate[at].astype(jnp.float32) + t_base[at]
        row_blocks(one)
        done = pltpu.make_async_copy(t_out, out_tok, tok_l.at[2])
        done.start()
        return done

    def meet(k, part, n):
        if k > 0:
            slot = part * 4 + n
            own_copies[k, part, n].wait()
            sets = hop(part, n)
            arrive(view(other[k], k, part, sets), core_s.at[slot, k], core_r.at[slot, k], twin_id)
            add_region(k, part, sets, [other[k].at[(slice(None),) * 5 + (part,)]])
        elif n == 0:
            own_copies[0, part].wait()
            theirs = other[0].at[:, :, :, part]
            arrive(theirs, core_s.at[part, 0], core_r.at[part, 0], twin_id)

            def one(i, carry):
                acc[0][1, 1, i, :, :, part] = acc[0][1, 1, i, :, :, part] + other[0][i, :, :, part]
                return carry

            lax.fori_loop(0, 4, one, 0)

    def ring(k, part, step, arriving):
        dim = order_of(part)[0]
        ahead = 3 - step - (1 if arriving else 0)
        for direction, sign in enumerate((1, -1)):
            half = direction if step == 1 else None
            sets = sets_of(part, 0, me[dim] + sign * ahead)
            land = lands[part, 0, k].at[direction]
            slot = part * 2 + step - 1
            sems = send.at[slot, direction, k], recv.at[slot, direction, k]
            target = device_at(moved(me, **{dim: sign}))
            here = view(land, k, None, sets, half)
            if arriving:
                arrive(here, *sems, target)
                add_region(k, part, sets, [land], half)
            else:
                go(view(acc[k], k, part, sets, half), here, *sems, target)

    def near(k, part, phase, arriving):
        order = order_of(part)
        dim, gone = order[phase], order[: phase + 1]
        mine = sets_of(part, phase, me[dim])
        sources = []
        for o in OTHERS[dim]:
            sems = near_s.at[part, phase - 1, o, k], near_r.at[part, phase - 1, o, k]
            target = device_at(moved(me, **{dim: o}))
            land = lands[part, phase, k].at[o - 1]
            here = view(land, k, None, mine, None, gone)
            if arriving:
                arrive(here, *sems, target)
                sources.append(land)
            else:
                go(view(acc[k], k, part, sets_of(part, phase, me[dim] + o)), here, *sems, target)
        if arriving:
            add_region(k, part, mine, sources, None, gone)

    pairs = [(k, part) for k in (1, 2, 0) for part in range(3)]
    for k, part in pairs:
        meet(k, part, 0)
        ring(k, part, 1, False)
    tok_cross()
    v_c[c] = gv[...]
    vec_start(0)

    def vec_next(n):
        total = vec_finish(n)
        if n < 3:
            vec_lands[n + 1][me[vec_dims[n + 1]]] = total
            vec_start(n + 1)
        else:
            out_v[...] = total

    for k, part in pairs:
        meet(k, part, 1)
        meet(k, part, 2)
        ring(k, part, 1, True)
        ring(k, part, 2, False)
    vec_next(0)
    for k, part in pairs:
        meet(k, part, 3)
    vec_next(1)
    tok_theirs()
    vec_next(2)
    for k, part in pairs:
        ring(k, part, 2, True)
        near(k, part, 1, False)
    vec_next(3)
    tok_done = tok_mine()
    for k, part in pairs:
        near(k, part, 1, True)
        near(k, part, 2, False)
    for k, part in pairs:
        near(k, part, 2, True)

    for k in range(2):
        for part in range(3):
            stage[pl.ds(8 * part, 8), :] = acc[k][yp, q, x, zh, m, part].astype(jnp.float32)
        for owner in range(4):
            rows[k, owner] = stage[pl.ds(6 * owner, 6), :]
    for part in range(3):
        tall_f[part] = acc[2][x, zh, m, yp, q, part].astype(jnp.float32)

    def cols_at(at):
        return pl.ds(pl.multiple_of((lax.rem(at["y"], 2) * 2 + lax.rem(at["z"], 2)) * 768 + at["c"] * HALF, 128), HALF)

    def owner_of(at):
        return lax.rem(at["y"], 2) * 2 + at["c"]

    for k, out in enumerate((out0, out1)):
        for n, mate in enumerate(mates):
            go(rows.at[k, owner_of(mate)], out.at[:, cols_at(me)], fin_s.at[k, n], fin_r.at[k, n], device_at(mate))
    kept = [
        pltpu.make_async_copy(rows.at[k, owner_of(me)], out.at[:, cols_at(me)], fin_s.at[k, 7])
        for k, out in enumerate((out0, out1))
    ]
    for cp in kept:
        cp.start()
    stays = c == q
    half_at = [pl.ds(pl.multiple_of(a * HALF, 128), HALF) for a in (c, 1 - c)]
    t_self = pltpu.make_async_copy(tall_f, out2.at[:, :, half_at[0]], t_s.at[0])
    there_same, there_cross = device_at(other_q(me)), device_at(other_q(twin))
    t_twin = sending(tall_f, out2.at[:, :, half_at[0]], t_s.at[0], t_r.at[0], twin_id)
    t_same = sending(tall_f, out2.at[:, :, half_at[0]], t_s.at[1], t_r.at[1], there_same)
    t_cross = sending(tall_f, out2.at[:, :, half_at[0]], t_s.at[1], t_r.at[2], there_cross)

    @pl.when(stays)
    def _():
        t_self.start()
        t_same.start()

    @pl.when(jnp.logical_not(stays))
    def _():
        t_twin.start()
        t_cross.start()

    for k, out in enumerate((out0, out1)):
        for n, mate in enumerate(mates):
            arrive(out.at[:, cols_at(mate)], fin_s.at[k, n], fin_r.at[k, n], device_at(mate))

    @pl.when(stays)
    def _():
        arrive(out2.at[:, :, half_at[1]], t_s.at[0], t_r.at[0], twin_id)
        t_self.wait()
        t_same.wait_send()

    @pl.when(jnp.logical_not(stays))
    def _():
        arrive(out2.at[:, :, half_at[0]], t_s.at[1], t_r.at[1], there_same)
        arrive(out2.at[:, :, half_at[1]], t_s.at[1], t_r.at[2], there_cross)
        t_twin.wait_send()
        t_cross.wait_send()

    for cp in kept:
        cp.wait()
    tok_done.wait()
    for cp in sent:
        cp.wait_send()


def reduce_all(g0, g0_other, g1, g2, gv, dx, base):
    bf, f32, dma = jnp.bfloat16, jnp.float32, pltpu.SemaphoreType.DMA
    lands = []
    for part in range(3):
        order = ORDERS[part][::-1]
        for phase in range(3):
            size = dict(DIM_SIZE)
            for dim, names in (("x", ("x",)), ("y", ("m", "yp")), ("z", ("zh", "q"))):
                if phase > 0 and dim in order[: phase + 1]:
                    for name in names:
                        size[name] = 1
            count = 2 if phase == 0 else EXTENT[order[phase]] - 1
            lands += [pltpu.VMEM((count, *(size[d] for d in dims_of(k)), 8, HALF), bf) for k in STREAMS]
    whole = [pltpu.VMEM(WIDE, bf), pltpu.VMEM(TALL, bf)]
    return pl.pallas_call(
        reduce_kernel,
        name="reduce_all",
        out_shape=(
            jax.ShapeDtypeStruct((6, 3072), f32),
            jax.ShapeDtypeStruct((6, 3072), f32),
            jax.ShapeDtypeStruct((3, 8, 768), f32),
            jax.ShapeDtypeStruct((16, 768), f32),
            jax.ShapeDtypeStruct((TILE, 768), f32),
        ),
        in_specs=[ANY_SPACE, ANY_SPACE, ANY_SPACE, ANY_SPACE, IN_VMEM, ANY_SPACE, ANY_SPACE],
        out_specs=(ANY_SPACE, ANY_SPACE, ANY_SPACE, IN_VMEM, ANY_SPACE),
        scratch_shapes=[
            pltpu.VMEM(WIDE, bf), *whole, pltpu.VMEM((4, 4, 2, 3, 8, HALF), bf), *whole, *lands,
            pltpu.VMEM((24, HALF), f32),
            pltpu.VMEM((2, 4, 6, HALF), f32),
            pltpu.VMEM((3, 8, HALF), f32),
            pltpu.VMEM((2, 16, 768), f32),
            pltpu.VMEM((4, 16, 768), f32),
            pltpu.VMEM((4, 16, 768), f32),
            pltpu.VMEM((8, 16, 768), f32),
            pltpu.VMEM((3, 2, TILE, 768), bf),
            pltpu.VMEM((3, 2, TILE, 768), bf),
            pltpu.VMEM((2, 2, TILE, 768), bf),
            pltpu.VMEM((TILE, 768), bf),
            pltpu.VMEM((TILE, 768), bf),
            pltpu.VMEM((TILE, 768), f32),
            pltpu.VMEM((TILE, 768), f32),
            dma((12, 3)), dma((12, 3)), dma((12, 3)), dma((3, 2, 8, 3)), dma((3, 2, 8, 3)), dma((6, 2, 3)), dma((6, 2, 3)),
            dma((2, 8)), dma((2, 7)),
            dma((2,)), dma((3,)), dma((4, 8)), dma((4, 8)), dma((6,)), dma((6,)), dma((3,)),
        ],
        compiler_params=pltpu.CompilerParams(collective_id=2, has_side_effects=True, vmem_limit_bytes=60 << 20),
    )(g0, g0_other, g1, g2, gv, dx, base)


def to_tokens_kernel(heads, rows, send, recv, local):
    me = place()
    c = me["c"]
    twin = device_at(moved(me, c=1))
    mine, other = (pl.ds(pl.multiple_of(a * HALF, 128), HALF) for a in (c, 1 - c))
    greet((twin,))
    out = sending(heads.at[1 - c], rows.at[:, mine], send.at[0], recv.at[0], twin)
    out.start()
    kept = pltpu.make_async_copy(heads.at[c], rows.at[:, mine], local.at[0])
    kept.start()
    kept.wait()
    sending(heads.at[c], rows.at[:, other], send.at[0], recv.at[0], twin).wait_recv()
    out.wait_send()


def to_heads_kernel(rows, heads, send, recv, local):
    me = place()
    c = me["c"]
    twin = device_at(moved(me, c=1))
    mine, other = (pl.ds(pl.multiple_of(a * HALF, 128), HALF) for a in (c, 1 - c))
    greet((twin,))
    out = sending(rows.at[:, other], heads.at[c], send.at[0], recv.at[0], twin)
    out.start()
    kept = pltpu.make_async_copy(rows.at[:, mine], heads.at[c], local.at[0])
    kept.start()
    kept.wait()
    sending(rows.at[:, mine], heads.at[1 - c], send.at[0], recv.at[0], twin).wait_recv()
    out.wait_send()


def swap(kernel, name, shape, number, array):
    return pl.pallas_call(
        kernel,
        name=name,
        out_shape=jax.ShapeDtypeStruct(shape, array.dtype),
        in_specs=[ANY_SPACE],
        out_specs=IN_VMEM,
        scratch_shapes=[pltpu.SemaphoreType.DMA((1,))] * 3,
        compiler_params=pltpu.CompilerParams(collective_id=number, has_side_effects=True, vmem_limit_bytes=58 << 20),
    )(array)


def dot32(a, b):
    return jnp.dot(a, b, preferred_element_type=jnp.float32)


def lanes_low(rows):
    return lax.broadcasted_iota(jnp.int32, (rows, 128), 1) < HEAD_DIM


def across_lanes(a, b):
    return lax.dot_general(a, b, (((1,), (1,)), ((), ())), preferred_element_type=jnp.float32)


def flipped(a):
    return jnp.swapaxes(a, 0, 1)


def project_kernel(plan, x_ref, w_ref, bq_ref, bv_ref, q_ref, kv_ref):
    t = pl.program_id(0)
    x = x_ref[0]
    for i in range(2):
        @pl.when(t == plan[1 + i])
        def _():
            q_ref[i] = (dot32(x, w_ref[0, 0]) + bq_ref[0]).astype(jnp.bfloat16)

    @pl.when(jnp.logical_and(t >= plan[7], t < plan[8]))
    def _():
        kv_ref[0, 0] = dot32(x, w_ref[0, 1]).astype(jnp.bfloat16)
        kv_ref[1, 0] = (dot32(x, w_ref[0, 2]) + bv_ref[0]).astype(jnp.bfloat16)


def project(plan, window, first, bias_q, bias_v):
    half = pl.BlockSpec((1, 1, HALF), lambda t, p: (p[0], 0, 0))
    return pl.pallas_call(
        project_kernel,
        name="project",
        grid_spec=pltpu.PrefetchScalarGridSpec(
            num_scalar_prefetch=1,
            grid=(12,),
            in_specs=[
                pl.BlockSpec((1, TILE, 768), lambda t, p: (t, 0, 0)),
                pl.BlockSpec((1, 4, 768, HALF), lambda t, p: (p[0], 0, 0, 0)),
                half, half,
            ],
            out_specs=[
                pl.BlockSpec((2, TILE, HALF), lambda t, p: (0, 0, 0)),
                pl.BlockSpec((2, 1, TILE, HALF), lambda t, p: (0, t, 0, 0)),
            ],
        ),
        out_shape=(
            jax.ShapeDtypeStruct((2, TILE, HALF), jnp.bfloat16),
            jax.ShapeDtypeStruct((2, 12, TILE, HALF), jnp.bfloat16),
        ),
        compiler_params=pltpu.CompilerParams(vmem_limit_bytes=58 << 20),
    )(plan, window, first, bias_q, bias_v)


def attend_kernel(plan, q_docs, k_docs, q_ref, kv, o_ref, lse_ref, top, total, acc):
    i = pl.program_id(1)
    low = lanes_low(TILE)
    q = q_ref[0]
    none = jnp.zeros_like(q)
    q_heads = (jnp.where(low, q, none), jnp.where(low, none, q))
    docs = q_docs[0]
    top[...] = jnp.full_like(top, BOTTOM)
    total[...] = jnp.zeros_like(total)
    acc[...] = jnp.zeros_like(acc)
    scale = HEAD_DIM ** -0.5 * LOG2E

    def step(j, carry):
        k, v = kv[0, j], flipped(kv[1, j])
        same = docs == k_docs[j]
        for head in range(2):
            rows = slice(head * HEAD_DIM, (head + 1) * HEAD_DIM)
            s = jnp.where(same, across_lanes(k, q_heads[head]) * scale, BOTTOM)
            old = top[head]
            new = jnp.maximum(old, jnp.max(s, axis=0, keepdims=True))
            fade = jnp.exp2(old - new)
            p = jnp.exp2(s - new)
            total[head] = total[head] * fade + jnp.sum(p, axis=0, keepdims=True)
            top[head] = new
            acc[rows] = acc[rows] * fade + dot32(v[rows], p.astype(jnp.bfloat16))
        return carry

    lax.fori_loop(plan[3 + 2 * i], plan[4 + 2 * i], step, 0)
    for head in range(2):
        rows = slice(head * HEAD_DIM, (head + 1) * HEAD_DIM)
        acc[rows] = acc[rows] / total[head]
        lse_ref[0, 0, pl.ds(head, 1)] = top[head] + jnp.log2(total[head])
    o_ref[0] = flipped(acc[...]).astype(jnp.bfloat16)


OWN_PAIR = pl.BlockSpec((1, TILE, 128), lambda p, i, b: (i, 0, p))
WINDOW_PAIR = pl.BlockSpec((2, 12, TILE, 128), lambda p, i, b: (0, 0, 0, p))
STATS = pl.BlockSpec((1, 1, 2, TILE), lambda p, i, b: (p, i, 0, 0))
DOC_SPECS = [
    pl.BlockSpec((1, 1, TILE), lambda p, i, b: (i, 0, 0)),
    pl.BlockSpec((12, TILE, 1), lambda p, i, b: (0, 0, 0)),
]


def attend(plan, q_docs, k_docs, q_heads, kv):
    return pl.pallas_call(
        attend_kernel,
        name="attend",
        grid_spec=pltpu.PrefetchScalarGridSpec(
            num_scalar_prefetch=1,
            grid=(3, 2),
            in_specs=[*DOC_SPECS, OWN_PAIR, WINDOW_PAIR],
            out_specs=[OWN_PAIR, STATS],
            scratch_shapes=[
                pltpu.VMEM((2, 1, TILE), jnp.float32),
                pltpu.VMEM((2, 1, TILE), jnp.float32),
                pltpu.VMEM((128, TILE), jnp.float32),
            ],
        ),
        out_shape=(
            jax.ShapeDtypeStruct((2, TILE, HALF), jnp.bfloat16),
            jax.ShapeDtypeStruct((3, 2, 2, TILE), jnp.float32),
        ),
        compiler_params=pltpu.CompilerParams(vmem_limit_bytes=58 << 20),
    )(plan, q_docs, k_docs, q_heads, kv)


def attend_back_kernel(plan, q_docs, k_docs, q_ref, do_ref, o_ref, lse_ref, kv, dq_ref, dkv_ref, dkv, dq):
    i = pl.program_id(1)
    low = lanes_low(TILE)

    @pl.when(i == 0)
    def _():
        dkv[...] = jnp.zeros_like(dkv)

    q, d_out = q_ref[0], do_ref[0]
    none = jnp.zeros_like(q)
    q_heads = (jnp.where(low, q, none), jnp.where(low, none, q))
    do_heads = (jnp.where(low, d_out, none), jnp.where(low, none, d_out))
    prod = d_out.astype(jnp.float32) * o_ref[0].astype(jnp.float32)
    first = lax.broadcasted_iota(jnp.int32, (8, 128), 0)
    halves = lax.broadcasted_iota(jnp.int32, (8, 128), 1) // HEAD_DIM
    deltas = lax.dot_general(
        (first == halves).astype(jnp.float32), prod, (((1,), (1,)), ((), ())),
        precision=lax.Precision.HIGHEST, preferred_element_type=jnp.float32,
    )
    deltas = (deltas[0:1], deltas[1:2])
    lses = (lse_ref[0, 0, 0:1], lse_ref[0, 0, 1:2])
    docs = q_docs[0]
    dq[...] = jnp.zeros_like(dq)
    scale = HEAD_DIM ** -0.5 * LOG2E

    def step(j, carry):
        k, v = kv[0, j], kv[1, j]
        k_flip = flipped(k)
        same = docs == k_docs[j]
        dk, dv = [], []
        for head in range(2):
            rows = slice(head * HEAD_DIM, (head + 1) * HEAD_DIM)
            s = across_lanes(k, q_heads[head]) * scale
            p = jnp.where(same, jnp.exp2(s - lses[head]), 0.0)
            dp = across_lanes(v, do_heads[head])
            ds = (p * (dp - deltas[head])).astype(jnp.bfloat16)
            dq[rows] += dot32(k_flip[rows], ds)
            dk.append(dot32(ds, q_heads[head]))
            dv.append(dot32(p.astype(jnp.bfloat16), do_heads[head]))
        dkv[0, j] += dk[0] + dk[1]
        dkv[1, j] += dv[0] + dv[1]
        return carry

    lax.fori_loop(plan[3 + 2 * i], plan[4 + 2 * i], step, 0)
    dq_ref[0] = flipped(dq[...] * HEAD_DIM ** -0.5).astype(jnp.bfloat16)

    @pl.when(i == 1)
    def _():
        dkv_ref[0] = (dkv[0] * HEAD_DIM ** -0.5).astype(jnp.bfloat16)
        dkv_ref[1] = dkv[1].astype(jnp.bfloat16)


def attend_back(plan, q_docs, k_docs, q_heads, d_heads, o_heads, lse, kv):
    return pl.pallas_call(
        attend_back_kernel,
        name="attend_back",
        grid_spec=pltpu.PrefetchScalarGridSpec(
            num_scalar_prefetch=1,
            grid=(3, 2),
            in_specs=[*DOC_SPECS, OWN_PAIR, OWN_PAIR, OWN_PAIR, STATS, WINDOW_PAIR],
            out_specs=[OWN_PAIR, WINDOW_PAIR],
            scratch_shapes=[
                pltpu.VMEM((2, 12, TILE, 128), jnp.float32),
                pltpu.VMEM((128, TILE), jnp.float32),
            ],
        ),
        out_shape=(
            jax.ShapeDtypeStruct((2, TILE, HALF), jnp.bfloat16),
            jax.ShapeDtypeStruct((2, 12, TILE, HALF), jnp.bfloat16),
        ),
        compiler_params=pltpu.CompilerParams(vmem_limit_bytes=58 << 20),
    )(plan, q_docs, k_docs, q_heads, d_heads, o_heads, lse, kv)


def project_back_kernel(plan, x_ref, w_ref, dq_ref, dkv_ref, dw_ref, dx_ref, sums_ref, dw, sums):
    t = pl.program_id(0)

    @pl.when(t == 0)
    def _():
        dw[...] = jnp.zeros_like(dw)
        sums[...] = jnp.zeros_like(sums)

    used = jnp.logical_and(t >= plan[7], t < plan[8])

    @pl.when(used)
    def _():
        x_flip = flipped(x_ref[0])
        dk, dv = dkv_ref[0, 0], dkv_ref[1, 0]
        dw[1] += dot32(x_flip, dk)
        dw[2] += dot32(x_flip, dv)
        sums[1:2] += jnp.sum(dv.astype(jnp.float32), axis=0, keepdims=True)
        dx = across_lanes(dk, w_ref[0, 1]) + across_lanes(dv, w_ref[0, 2])
        dx_ref[0] = dx.astype(jnp.bfloat16)
        for i in range(2):
            @pl.when(t == plan[1 + i])
            def _():
                dq = dq_ref[i]
                dw[0] += dot32(x_flip, dq)
                sums[0:1] += jnp.sum(dq.astype(jnp.float32), axis=0, keepdims=True)
                dx_ref[0] = (dx + across_lanes(dq, w_ref[0, 0])).astype(jnp.bfloat16)

    @pl.when(jnp.logical_not(used))
    def _():
        dx_ref[...] = jnp.zeros_like(dx_ref)

    @pl.when(t == 11)
    def _():
        dw_ref[...] = dw[...].astype(jnp.bfloat16)
        sums_ref[...] = sums[...]


def project_back(plan, window, first, dq, dkv):
    return pl.pallas_call(
        project_back_kernel,
        name="project_back",
        grid_spec=pltpu.PrefetchScalarGridSpec(
            num_scalar_prefetch=1,
            grid=(12,),
            in_specs=[
                pl.BlockSpec((1, TILE, 768), lambda t, p: (t, 0, 0)),
                pl.BlockSpec((1, 4, 768, HALF), lambda t, p: (p[0], 0, 0, 0)),
                pl.BlockSpec((2, TILE, HALF), lambda t, p: (0, 0, 0)),
                pl.BlockSpec((2, 1, TILE, HALF), lambda t, p: (0, t, 0, 0)),
            ],
            out_specs=[
                pl.BlockSpec((3, 768, HALF), lambda t, p: (0, 0, 0)),
                pl.BlockSpec((1, TILE, 768), lambda t, p: (t, 0, 0)),
                pl.BlockSpec((8, HALF), lambda t, p: (0, 0)),
            ],
            scratch_shapes=[pltpu.VMEM((3, 768, HALF), jnp.float32), pltpu.VMEM((8, HALF), jnp.float32)],
        ),
        out_shape=(
            jax.ShapeDtypeStruct((3, 768, HALF), jnp.bfloat16),
            jax.ShapeDtypeStruct((12, TILE, 768), jnp.bfloat16),
            jax.ShapeDtypeStruct((8, HALF), jnp.float32),
        ),
        compiler_params=pltpu.CompilerParams(vmem_limit_bytes=58 << 20),
    )(plan, window, first, dq, dkv)


def norm_parts(resid):
    centred = resid - jnp.mean(resid, axis=1, keepdims=True)
    inverse = lax.rsqrt(jnp.mean(centred * centred, axis=1, keepdims=True) + NORM_EPS)
    return centred * inverse, inverse


def norm_back(upstream, gain, n, inverse):
    e = upstream * gain
    return inverse * (e - jnp.mean(e, axis=1, keepdims=True) - n * jnp.mean(e * n, axis=1, keepdims=True))


def row_sum(a):
    return jnp.sum(a, axis=0, keepdims=True)


def mlp_kernel(
    att_ref, tok_ref, cot_ref, rows, bias_in, first, second, third,
    out_ref, d_one_ref, d_att_ref, dwo_ref, dw_in_ref, dw_down_ref, sums_ref, sums_in_ref,
    w_out, w_in, w_down, n_one, low, low_flip, slope, active, wide, sem,
):
    f32, bf = jnp.float32, jnp.bfloat16
    loads = [pltpu.make_async_copy(first.at[:, 3], w_out, sem.at[0])]
    loads += [pltpu.make_async_copy(second, w_in, sem.at[1]), pltpu.make_async_copy(third, w_down, sem.at[2])]
    for cp in loads:
        cp.start()

    def row(n):
        return rows[n : n + 1]

    halves = (slice(0, HALF), slice(HALF, 768))
    loads[0].wait()
    att = att_ref[...]
    for h in range(2):
        wide[:, halves[h]] = dot32(att, w_out[h])
    one, inverse_one = norm_parts(tok_ref[...].astype(f32) + (wide[...] + row(2)))
    n_one[...] = one
    normed = one * row(3) + row(4)
    low[...] = normed.astype(bf)
    low_flip[...] = flipped(low[...])
    wide[...] = normed + row(5)
    loads[1].wait()
    loads[2].wait()

    def up(m, carry):
        h = dot32(low[...], w_in[lax.rem(m, 2), m // 2]) + bias_in[m]
        cdf = 0.5 * (1.0 + lax.erf(h * 0.7071067811865476))
        slope[m] = cdf + h * jnp.exp(h * h * -0.5) * 0.3989422804014327
        a = (h * cdf).astype(bf)
        active[m] = flipped(a)
        for k in range(2):
            wide[:, halves[k]] += dot32(a, w_down[k, m])
        return carry

    lax.fori_loop(0, 8, up, 0)
    two, inverse_two = norm_parts(wide[...])
    out_ref[...] = (two * row(6) + row(7)).astype(bf)
    upstream = cot_ref[...].astype(f32)
    sums_ref[0:2] = jnp.zeros((2, 768), f32)
    sums_ref[6:7] = row_sum(upstream * two)
    sums_ref[7:8] = row_sum(upstream)
    d_two = norm_back(upstream, row(6), two, inverse_two)
    sums_ref[5:6] = row_sum(d_two)
    d_low = d_two.astype(bf)
    wide[...] = d_two

    def down(m, carry):
        d_active = None
        for k in range(2):
            d_half = d_low[:, halves[k]]
            dw_down_ref[k, m] = dot32(active[m], d_half).astype(bf)
            part = across_lanes(d_half, w_down[k, m])
            d_active = part if d_active is None else d_active + part
        d_hidden = (d_active * slope[m]).astype(bf)
        sums_in_ref[m] = row_sum(d_hidden.astype(f32))
        dw_in_ref[lax.rem(m, 2), m // 2] = dot32(low_flip[...], d_hidden).astype(bf)
        wide[...] += across_lanes(d_hidden, w_in[lax.rem(m, 2), m // 2])
        return carry

    lax.fori_loop(0, 8, down, 0)
    d_normed = wide[...]
    one = n_one[...]
    sums_ref[3:4] = row_sum(d_normed * one)
    sums_ref[4:5] = row_sum(d_normed)
    d_one = norm_back(d_normed, row(3), one, inverse_one)
    d_one_ref[...] = d_one
    sums_ref[2:3] = row_sum(d_one)
    d_low = d_one.astype(bf)
    att_flip = flipped(att_ref[...])
    d_att = None
    for h in range(2):
        d_half = d_low[:, halves[h]]
        dwo_ref[h] = dot32(att_flip, d_half).astype(bf)
        part = across_lanes(d_half, w_out[h])
        d_att = part if d_att is None else d_att + part
    d_att_ref[...] = d_att.astype(bf)


def mlp(att, tokens, cotangent, rows, bias_in, first, second, third):
    f32, bf = jnp.float32, jnp.bfloat16
    return pl.pallas_call(
        mlp_kernel,
        name="mlp",
        in_specs=[IN_VMEM] * 5 + [ANY_SPACE] * 3,
        out_specs=(IN_VMEM,) * 8,
        out_shape=(
            jax.ShapeDtypeStruct((TILE, 768), bf),
            jax.ShapeDtypeStruct((TILE, 768), f32),
            jax.ShapeDtypeStruct((TILE, 768), bf),
            jax.ShapeDtypeStruct((2, 768, HALF), bf),
            jax.ShapeDtypeStruct((2, 4, 768, HALF), bf),
            jax.ShapeDtypeStruct((2, 8, HALF, HALF), bf),
            jax.ShapeDtypeStruct((8, 768), f32),
            jax.ShapeDtypeStruct((8, 1, HALF), f32),
        ),
        scratch_shapes=[
            pltpu.VMEM((2, 768, HALF), bf),
            pltpu.VMEM((2, 4, 768, HALF), bf),
            pltpu.VMEM((2, 8, HALF, HALF), bf),
            pltpu.VMEM((TILE, 768), f32),
            pltpu.VMEM((TILE, 768), bf),
            pltpu.VMEM((768, TILE), bf),
            pltpu.VMEM((8, TILE, HALF), f32),
            pltpu.VMEM((8, HALF, TILE), bf),
            pltpu.VMEM((TILE, 768), f32),
            pltpu.SemaphoreType.DMA((3,)),
        ],
        compiler_params=pltpu.CompilerParams(vmem_limit_bytes=58 << 20),
    )(att, tokens, cotangent, rows, bias_in, first, second, third)


def body(
    tokens, w_qkv, bias_q, bias_v, w_out, bias_out, gain_one, shift_one, w_in, bias_in,
    w_down, bias_down, gain_two, shift_two, doc_lengths, cotangent,
):
    shard, seq = lax.axis_index("shard"), lax.axis_index("seq")
    core = lax.rem(shard, 2)
    f32, bf = jnp.float32, jnp.bfloat16
    width = tokens.shape[1]
    stream_len = tokens.shape[0] * lax.axis_size("seq") * lax.axis_size("shard")

    positions = (shard // 2 - 1) * (4 * TILE) + jnp.arange(12 * TILE, dtype=jnp.int32)
    starts = jnp.cumsum(doc_lengths, dtype=jnp.int32) - doc_lengths
    counted = jnp.sum((positions[:, None] >= starts[None, :]).astype(jnp.int32), axis=1, dtype=jnp.int32) - 1
    docs = jnp.where(positions < stream_len, counted, stream_len).reshape(12, TILE)
    query_docs = lax.dynamic_slice(docs, (4 + seq, 0), (3, TILE))[::2]
    lower = jnp.sum((docs[None, :, -1] < query_docs[:, :1]).astype(jnp.int32), axis=1)
    upper = jnp.sum((docs[None, :, 0] <= query_docs[:, -1:]).astype(jnp.int32), axis=1)
    plan = jnp.stack([core, 4 + seq, 6 + seq, lower[0], upper[0], lower[1], upper[1], lower[0], upper[1]])
    query_docs, key_docs = query_docs.reshape(2, 1, TILE), docs.reshape(12, TILE, 1)

    vectors = (bias_q, bias_v, bias_out, gain_one, shift_one, bias_down, gain_two, shift_two)
    vec = jnp.concatenate(
        [
            jnp.stack(vectors).astype(f32),
            jnp.pad(bias_in.astype(f32).reshape(1, 24), ((0, 7), (0, 0))),
            jnp.zeros((8, 98), f32),
        ],
        axis=1,
    )
    cat = jnp.stack([jnp.concatenate([w_qkv, w_out], axis=1), w_in])
    first, second, third, vecs, window = gather(cat, w_down.reshape(3, 8, width), vec, tokens)
    first = first.reshape(2, 4, width, HALF)
    second = second.reshape(2, 4, width, HALF)
    third = third.reshape(2, 8, HALF, HALF)
    window = window.reshape(12, TILE, width)
    vecs = jnp.transpose(vecs, (4, 1, 2, 3, 0, 5)).reshape(8, 128, 128)
    rows = vecs[:, :, :6].reshape(8, width)
    hidden_bias = vecs[0, :, 6:30].reshape(8, 1, HALF)

    q_heads, kv = project(plan, window, first, rows[0].reshape(2, 1, HALF), rows[1].reshape(2, 1, HALF))
    o_heads, lse = attend(plan, query_docs, key_docs, q_heads, kv)
    attended = swap(to_tokens_kernel, "to_tokens", (TILE, width), 4, o_heads)
    layer_out, d_one, d_att, dw_out, dw_in, dw_down, sums, sums_in = mlp(
        attended, tokens, cotangent, rows, hidden_bias, first, second, third
    )
    d_heads = swap(to_heads_kernel, "to_heads", (2, TILE, HALF), 5, d_att)
    dq, dkv = attend_back(plan, query_docs, key_docs, q_heads, d_heads, o_heads, lse, kv)
    dw_qkv, dx, head_sums = project_back(plan, window, first, dq, dkv)

    mine = jnp.arange(2) == core
    dw_out_mine = lax.dynamic_index_in_dim(dw_out, core, 0)
    dw_out_other = lax.dynamic_index_in_dim(dw_out, 1 - core, 0, keepdims=False)
    grad_first = jnp.concatenate([dw_qkv, dw_out_mine], axis=0)
    both = jnp.where(mine[None, :, None], head_sums[:2, None], 0.0).reshape(2, width)
    vec_sums = jnp.concatenate([both, sums[2:], sums_in.reshape(4, width), jnp.zeros((4, width), f32)], axis=0)
    sum_first, sum_in, sum_down, sum_vec, grad_tokens = reduce_all(
        grad_first.reshape(WIDE), dw_out_other.reshape(4, 4, 2, 3, 8, HALF), dw_in.reshape(2, *WIDE), dw_down.reshape(2, *TALL), vec_sums,
        dx.reshape(3, 2, 2, TILE, width), d_one,
    )
    own = lax.dynamic_slice(sum_vec, (0, 6 * shard), (8, 6))
    own_in = lax.dynamic_slice(sum_vec[8:12].reshape(-1), (24 * shard,), (24,))
    return (
        layer_out, grad_tokens, sum_first[:, : 3 * width], own[0], own[1], sum_first[:, 3 * width :],
        own[2], own[3], own[4], sum_in, own_in, sum_down.reshape(24, width), own[5], own[6], own[7],
    )


def solution(mesh):
    both, own = P(("shard", "seq"), None), P("shard")
    rows = P("shard", None)
    return jax.shard_map(
        body,
        mesh=mesh,
        in_specs=(both, rows, own, own, rows, own, own, own, rows, own, rows, own, own, own, P(), both),
        out_specs=(both, both, rows, own, own, rows, own, own, own, rows, own, rows, own, own, own),
        check_vma=False,
    )
```

profile of v0, /device:TPU:55, one launch (start us, length us, event | category | flops | bytes accessed | tf_op | source)
XLA Modules:
  0.0 388.6 jit_solution(7122819057580113801)
XLA Ops:
  0.7 0.8 copy.39
  2.4 1.8 convert_reduce_fusion
  6.1 4.5 %stack.51.plan = s32[9]{0:T(128)} concatenate(s32[1]{0:T(128)} %bitcast, s32[1]{0:T(128)} %bitcast.1, s32[1]{0:T(128)} %bitcast.2, s32[1]{0:T(128)} %get-tuple-element.88, s32[1]{0:T(128)} %get-tuple-element.86, s32[1]{0:T(128)} %get-tuple-element.87, s32[1]{0:T(128)} %get-tuple-element.85, s32[1]{0:T(128)} %get-tuple-element.88, s32[1]{0:T(128)} %get-tuple-element.85), dimensions={0} | concatenate | bytes 72 | tf_op jit(solution)/shard_map/stack | solution.py:1215
  10.6 0.8 maximum_bitcast_fusion
  11.4 1.5 pad_maximum_fusion.1.cat_ref
  12.8 0.8 stack.63
  14.4 0.7 maximum_maximum_fusion.1.vec_ref
  15.0 95.9 %gather.1 = (bf16[2,2,2,4,4,2,3,8,384]{8,7,6,5,4,3,2,1,0:T(8,128)(2,1)}, bf16[2,2,2,4,4,2,3,8,384]{8,7,6,5,4,3,2,1,0:T(8,128)(2,1)}, bf16[2,4,4,2,2,2,3,8,384]{8...) custom-call(bf16[2,6,3072]{2,1,0:T(8,128)(2,1)} %pad_maximum_fusion.1.cat_ref, ...), custom_call_target="tpu_custom_call" | custom-call | tf_op jit(solution)/shard_map/gather/pallas_call | solution.py:353
  110.9 1.1 copy.41
  112.3 0.7 reshape_squeeze.12.bq_ref
  113.1 0.7 reshape_squeeze.13.bv_ref
  113.8 12.2 %project.1 = (bf16[2,256,384]{2,1,0:T(8,128)(2,1)}, bf16[2,12,256,384]{3,2,1,0:T(8,128)(2,1)}) custom-call(s32[9]{0:T(128)} %stack.51.plan, bf16[12,256,768]{2,1,0:T(8,128)(2,1)} %bitcast.52, bf16[2,4,768,384]{3,2,1,0:T(8,128)(2,1)} %bitcast.49, f32[2,1,384]{2,1,0:T(1,128)} %reshape_squeeze.12.bq_ref, f32[2,1,384]{2,1,0:T(1,128)} %reshape_squeeze.13.bv_ref), custom_call_target="tpu_custom_call" | custom-call | tf_op jit(solution)/shard_map/project/pallas_call | solution.py:837
  126.0 1.4 sub.28
  127.4 1.4 fusion.k_docs
  129.3 25.0 %attend.1 = (bf16[2,256,384]{2,1,0:T(8,128)(2,1)}, f32[3,2,2,256]{3,2,1,0:T(2,128)}) custom-call(s32[9]{0:T(128)} %stack.51.plan, s32[2,1,256]{2,1,0:T(1,128)} %reshape.169.q_docs, s32[12,256,1]{2,1,0:T(8,128)} %fusion.k_docs, bf16[2,256,384]{2,1,0:T(8,128)(2,1)} %get-tuple-element.45.q_ref, bf16[2,12,256,384]{3,2,1,0:T(8,128)(2,1)} %get-tuple-element.46.kv), custom_call_target="tpu_custom_call" | custom-call | tf_op jit(solution)/shard_map/attend/pallas_call | solution.py:906
  154.3 2.4 to_tokens.1.att_ref
  156.9 0.9 reshape.175.rows
  158.0 0.7 reshape_squeeze.14.bias_in
  158.7 27.4 %mlp.1 = (bf16[256,768]{1,0:T(8,128)(2,1)}, f32[256,768]{1,0:T(8,128)}, bf16[256,768]{1,0:T(8,128)(2,1)}, bf16[2,768,384]{2,1,0:T(8,128)(2,1)}, bf16[2,4,768,384...) custom-call(bf16[256,768]{1,0:T(8,128)(2,1)} %to_tokens.1.att_ref, ...), custom_call_target="tpu_custom_call" | custom-call | tf_op jit(solution)/shard_map/mlp/pallas_call | solution.py:1167
  186.1 2.6 to_heads.1.do_ref
  188.8 30.3 %attend_back.1 = (bf16[2,256,384]{2,1,0:T(8,128)(2,1)}, bf16[2,12,256,384]{3,2,1,0:T(8,128)(2,1)}) custom-call(s32[9]{0:T(128)} %stack.51.plan, s32[2,1,256]{2,1,0:T(1,128)} %reshape.169.q_docs, s32[12,256,1]{2,1,0:T(8,128)} %fusion.k_docs, bf16[2,256,384]{2,1,0:T(8,128)(2,1)} %get-tuple-element.45.q_ref, bf16[2,256,384]{2,1,0:T(8,128)(2,1)} %to_heads.1.do_ref, ...), custom_call_target="tpu_custom_call" | custom-call | tf_op jit(solution)/shard_map/attend_back/pallas_call | solution.py:981
  219.0 16.0 %project_back.1 = (bf16[3,768,384]{2,1,0:T(8,128)(2,1)}, bf16[12,256,768]{2,1,0:T(8,128)(2,1)}, f32[8,384]{1,0:T(8,128)}) custom-call(s32[9]{0:T(128)} %stack.51.plan, bf16[12,256,768]{2,1,0:T(8,128)(2,1)} %bitcast.53, bf16[2,4,768,384]{3,2,1,0:T(8,128)(2,1)} %bitcast.51, bf16[2,256,384]{2,1,0:T(8,128)(2,1)} %get-tuple-element.53.dq_ref, ...), custom_call_target="tpu_custom_call" | custom-call | tf_op jit(solution)/shard_map/project_back/pallas_call | solution.py:1040
  235.1 0.8 slice.97
  236.2 0.7 maximum_maximum_fusion.refs_4_
  236.9 1.0 constant_dynamic-slice_fusion.1
  237.9 1.7 pad_maximum_fusion
  239.5 140.1 %reduce_all.1 = (f32[6,3072]{1,0:T(8,128)}, f32[6,3072]{1,0:T(8,128)}, f32[3,8,768]{2,1,0:T(8,128)}, f32[16,768]{1,0:T(8,128)}, f32[256,768]{1,0:T(8,128)}) custom-call(bf16[2,2,4,4,2,3,8,384]{7,6,5,4,3,2,1,0:T(8,128)(2,1)} %bitcast.54, bf16[4,4,2,3,8,384]{5,4,3,2,1,0:T(8,128)(2,1)} %bitcast.63, bf16[2,2,2,4,4,2,3,8,384]{8,7,6,5,4,3,2,1,0:T(8,128)(2,1)} %bitcast.55, ...), custom_call_target="tpu_custom_call" | custom-call | tf_op jit(solution)/shard_map/reduce_all/pallas_call | solution.py:727
  379.7 1.6 slice.99
  381.3 0.7 slice.106
  382.6 1.3 slice.102
  383.9 0.8 constant_dynamic-slice_fusion
  385.3 2.1 copy.50
  (50 shorter events, 7.5 us)
Async XLA Ops:
  219.0 17.0 %copy-start.5 = (f32[8,1,384]{2,1,0:T(1,128)S(1)}, f32[8,1,384]{2,1,0:T(1,128)}, u32[]{:S(2)}) copy-start(f32[8,1,384]{2,1,0:T(1,128)} %get-tuple-element.61) | copy-start | bytes 36868
  219.0 17.1 %copy-start.4 = (f32[8,768]{1,0:T(8,128)S(1)}, f32[8,768]{1,0:T(8,128)}, u32[]{:S(2)}) copy-start(f32[8,768]{1,0:T(8,128)} %get-tuple-element.60) | copy-start | bytes 73732
  219.0 17.9 %copy-start.1 = (bf16[2,768,384]{2,1,0:T(8,128)(2,1)S(1)}, bf16[2,768,384]{2,1,0:T(8,128)(2,1)}, u32[]{:S(2)}) copy-start(bf16[2,768,384]{2,1,0:T(8,128)(2,1)} %get-tuple-element.56) | copy-start | bytes 3538948
  235.1 2.8 copy-start
  379.7 7.6 %copy-start.2 = (f32[6,3072]{1,0:T(8,128)S(1)}, f32[6,3072]{1,0:T(8,128)}, u32[]{:S(2)}) copy-start(f32[6,3072]{1,0:T(8,128)} %get-tuple-element.115) | copy-start | bytes 221188
  379.7 8.3 %copy-start.3 = (f32[3,8,768]{2,1,0:T(8,128)S(1)}, f32[3,8,768]{2,1,0:T(8,128)}, u32[]{:S(2)}) copy-start(f32[3,8,768]{2,1,0:T(8,128)} %get-tuple-element.68) | copy-start | bytes 221188
where the time goes:
time: 391 us; the launch traced here: 389 us
  Pallas kernels  352 us (90%)
  local copies, waits for them, and re-layouts  25.4 us (6%)
  other arithmetic  10.4 us (3%)
    pallas_call x1, Pallas kernels, reduce_all(): pl.pallas_call(reduce_kernel, name='reduce_all', out_shape=(jax.ShapeDtyp...  140 us
    pallas_call x1, Pallas kernels, gather(): pl.pallas_call(gather_kernel, name='gather', out_shape=(jax.ShapeDtypeStr...  95.9 us
    pallas_call x1, Pallas kernels, attend_back(): pl.pallas_call(attend_back_kernel, name='attend_back', grid_spec=pltpu.Pr...  30.3 us
    pallas_call x1, Pallas kernels, mlp(): pl.pallas_call(mlp_kernel, name='mlp', in_specs=[IN_VMEM] * 5 + [ANY_SPAC...  27.4 us
    pallas_call x1, Pallas kernels, attend(): pl.pallas_call(attend_kernel, name='attend', grid_spec=pltpu.PrefetchScal...  25 us
    pallas_call x1, Pallas kernels, project_back(): pl.pallas_call(project_back_kernel, name='project_back', grid_spec=pltpu....  16 us
    pallas_call x1, Pallas kernels, project(): pl.pallas_call(project_kernel, name='project', grid_spec=pltpu.PrefetchSc...  12.2 us

commit v1 on v0

--- a/solution.py
+++ b/solution.py
@@ -180,11 +180,13 @@
         go(src, dst, tok_s.at[at], tok_r.at[at], target)
 
     tok_kept = pltpu.make_async_copy(tok_ref, window.at[1, c, q], local.at[3])
-    tok_kept.start()
-    tok_go(tok_ref, window.at[1, c, q], 0, partner)
-    tok_go(tok_ref, window.at[0, c, q], 1, after)
-    tok_go(tok_ref, window.at[2, c, q], 2, before)
-    tok_go(tok_ref, window.at[1, c, q], 3, twin_id)
+
+    def tok_start():
+        tok_kept.start()
+        tok_go(tok_ref, window.at[1, c, q], 0, partner)
+        tok_go(tok_ref, window.at[0, c, q], 1, after)
+        tok_go(tok_ref, window.at[2, c, q], 2, before)
+        tok_go(tok_ref, window.at[1, c, q], 3, twin_id)
 
     def tok_forward():
         theirs = window.at[1, c, 1 - q]
@@ -306,13 +308,14 @@
         for part in range(3):
             near(k, part, 0, True)
             near(k, part, 1, False)
-    tok_forward()
+    tok_start()
     vec_wait(0)
     vec_start(1)
     for k in STREAMS:
         for part in range(3):
             near(k, part, 1, True)
             ring(k, part, 1, False)
+    tok_forward()
     for k in STREAMS:
         for part in range(3):
             share(k, part, sets_at(part, 2, me[ORDERS[part][2]]), None, part)
@@ -370,22 +373,24 @@
             dma((15, 3)), dma((15, 3)),
             dma((4, 3)), dma((4, 3)), dma((11,)), dma((11,)),
         ],
-        compiler_params=pltpu.CompilerParams(collective_id=1, has_side_effects=True, vmem_limit_bytes=58 << 20),
+        compiler_params=pltpu.CompilerParams(collective_id=1, has_side_effects=True),
     )(cat, down, vec, tokens)
 
 
-def reduce_kernel(*refs):
-    (g0, g0_other, g1, g2, gv, dx, base, out0, out1, out2, out_v, out_tok) = refs[:12]
+def back_kernel(*refs):
+    (q_docs, k_docs, q_ref, do_ref, o_ref, lse_ref, gv, kv_hbm, window_hbm, first, dwo, g1, g2, base) = refs[:14]
+    (out0, out1, out2, out_v, out_tok) = refs[14:19]
     grads = (None, g1, g2)
-    refs = refs[12:]
+    refs = refs[19:]
     acc, other, refs = refs[:3], refs[3:6], refs[6:]
     lands = {}
     for n, (part, phase, k) in enumerate((a, b, k) for a in range(3) for b in range(3) for k in STREAMS):
         lands[part, phase, k] = refs[n]
     refs = refs[27:]
     (
-        stage, rows, tall_f, v_c, v_x, v_y, v_z, t_acc, t_in, t_land, t_part, t_mate, t_base, t_out,
-        local, core_s, core_r, near_s, near_r, send, recv, fin_s, fin_r, t_s, t_r, vec_s, vec_r, tok_s, tok_r, tok_l,
+        stage, rows, tall_f, v_c, v_x, v_y, v_z, t_all, t_in, t_land, t_part, t_mate, t_base,
+        kv, window, w_heads, dkv_all, dkv, dq_all, dq_acc, dw, q_rows, v_rows,
+        local, core_s, core_r, near_s, near_r, send, recv, fin_s, fin_r, t_s, t_r, vec_s, vec_r, tok_s, tok_r, tok_l, load,
     ) = refs
     me = place()
     c, x, y, z = me["c"], me["x"], me["y"], me["z"]
@@ -477,21 +482,22 @@
         kept.start()
         own_copies[k, part, n] = kept
 
-    for part in range(3):
-        go(g0_other.at[:, :, :, part], other[0].at[:, :, :, part], core_s.at[part, 0], core_r.at[part, 0], twin_id)
-        whole = (slice(None),) * 5 + (part,)
-        own_copies[0, part] = pltpu.make_async_copy(g0.at[whole], acc[0].at[whole], local.at[part, 0])
-        own_copies[0, part].start()
+    loads = [
+        pltpu.make_async_copy(kv_hbm, kv, load.at[0]),
+        pltpu.make_async_copy(first.at[c, pl.ds(0, 3)], w_heads, load.at[1]),
+        pltpu.make_async_copy(window_hbm, window, load.at[2]),
+        pltpu.make_async_copy(dwo.at[c], acc[0].at[1, 1], load.at[3]),
+        pltpu.make_async_copy(base, t_base, load.at[4]),
+    ]
+    loads[0].start()
     for n in range(4):
         for k in (1, 2):
             for part in range(3):
                 cross(k, part, n)
 
-    go(dx.at[:, 1 - c], t_in, tok_s.at[0], tok_r.at[0], twin_id)
-    tok_kept = pltpu.make_async_copy(dx.at[:, c], t_acc, tok_l.at[0])
-    tok_kept.start()
-    base_kept = pltpu.make_async_copy(base, t_base, tok_l.at[1])
-    base_kept.start()
+    for cp in loads[1:]:
+        cp.start()
+    go(dwo.at[1 - c], other[0], core_s.at[0, 0], core_r.at[0, 0], twin_id)
 
     vec_lands = (v_c, v_x, v_y, v_z)
     vec_dims = ("c", "x", "y", "z")
@@ -516,23 +522,27 @@
     def row_blocks(fn):
         lax.fori_loop(0, TILE // 32, lambda r, carry: (fn(pl.ds(pl.multiple_of(r * 32, 32), 32)), carry)[1], 0)
 
-    def tok_cross():
-        tok_kept.wait()
-        arrive(t_in, tok_s.at[0], tok_r.at[0], twin_id)
+    def tok_twin(group, at):
+        go(t_all.at[1 - c, group], t_in.at[group], tok_s.at[at], tok_r.at[at], twin_id)
+
+    def tok_edges():
+        for n, (group, at) in enumerate(((0, 0), (2, 6))):
+            arrive(t_in.at[group], tok_s.at[at], tok_r.at[at], twin_id)
         for n, h in enumerate((1 - q, q)):
-            for r in (0, 2):
+            for group in (0, 2):
                 def one(at):
-                    t_acc[r, h, at] = t_acc[r, h, at] + t_in[r, h, at]
+                    t_all[c, group, h, at] = t_all[c, group, h, at] + t_in[group, h, at]
                 row_blocks(one)
-            go(t_acc.at[0, h], t_land.at[1, h], tok_s.at[1 + n], tok_r.at[1 + n], before)
-            go(t_acc.at[2, h], t_land.at[0, h], tok_s.at[3 + n], tok_r.at[3 + n], after)
+            go(t_all.at[c, 0, h], t_land.at[1, h], tok_s.at[1 + n], tok_r.at[1 + n], before)
+            go(t_all.at[c, 2, h], t_land.at[0, h], tok_s.at[3 + n], tok_r.at[3 + n], after)
 
     def tok_total(h, at):
         f = jnp.float32
-        return t_acc[1, h, at].astype(f) + t_in[1, h, at].astype(f) + t_land[0, h, at].astype(f) + t_land[1, h, at].astype(f)
+        return t_all[c, 1, h, at].astype(f) + t_in[1, h, at].astype(f) + t_land[0, h, at].astype(f) + t_land[1, h, at].astype(f)
 
     def tok_theirs():
         h = 1 - q
+        arrive(t_in.at[1], tok_s.at[7], tok_r.at[7], twin_id)
         arrive(t_land.at[1, h], tok_s.at[1], tok_r.at[1], after)
         arrive(t_land.at[0, h], tok_s.at[3], tok_r.at[3], before)
 
@@ -545,32 +555,31 @@
         arrive(t_land.at[1, q], tok_s.at[2], tok_r.at[2], after)
         arrive(t_land.at[0, q], tok_s.at[4], tok_r.at[4], before)
         arrive(t_mate, tok_s.at[5], tok_r.at[5], partner)
-        base_kept.wait()
+        loads[4].wait()
 
         def one(at):
-            t_out[at] = tok_total(q, at) + t_mate[at].astype(jnp.float32) + t_base[at]
+            t_base[at] = tok_total(q, at) + t_mate[at].astype(jnp.float32) + t_base[at]
         row_blocks(one)
-        done = pltpu.make_async_copy(t_out, out_tok, tok_l.at[2])
+        done = pltpu.make_async_copy(t_base, out_tok, tok_l.at[0])
         done.start()
         return done
 
     def meet(k, part, n):
-        if k > 0:
-            slot = part * 4 + n
-            own_copies[k, part, n].wait()
-            sets = hop(part, n)
-            arrive(view(other[k], k, part, sets), core_s.at[slot, k], core_r.at[slot, k], twin_id)
-            add_region(k, part, sets, [other[k].at[(slice(None),) * 5 + (part,)]])
-        elif n == 0:
-            own_copies[0, part].wait()
-            theirs = other[0].at[:, :, :, part]
-            arrive(theirs, core_s.at[part, 0], core_r.at[part, 0], twin_id)
-
-            def one(i, carry):
-                acc[0][1, 1, i, :, :, part] = acc[0][1, 1, i, :, :, part] + other[0][i, :, :, part]
-                return carry
-
-            lax.fori_loop(0, 4, one, 0)
+        slot = part * 4 + n
+        own_copies[k, part, n].wait()
+        sets = hop(part, n)
+        arrive(view(other[k], k, part, sets), core_s.at[slot, k], core_r.at[slot, k], twin_id)
+        add_region(k, part, sets, [other[k].at[(slice(None),) * 5 + (part,)]])
+
+    def meet_out():
+        loads[3].wait()
+        arrive(other[0], core_s.at[0, 0], core_r.at[0, 0], twin_id)
+
+        def one(i, carry):
+            acc[0][1, 1, i] = acc[0][1, 1, i] + other[0][i]
+            return carry
+
+        lax.fori_loop(0, 4, one, 0)
 
     def ring(k, part, step, arriving):
         dim = order_of(part)[0]
@@ -578,14 +587,14 @@
         for direction, sign in enumerate((1, -1)):
             half = direction if step == 1 else None
             sets = sets_of(part, 0, me[dim] + sign * ahead)
-            land = lands[part, 0, k].at[direction]
+            land = lands[part, 0, k].at[direction, step - 1]
             slot = part * 2 + step - 1
             sems = send.at[slot, direction, k], recv.at[slot, direction, k]
             target = device_at(moved(me, **{dim: sign}))
-            here = view(land, k, None, sets, half)
+            here = view(land, k, None, sets, half, (dim,))
             if arriving:
                 arrive(here, *sems, target)
-                add_region(k, part, sets, [land], half)
+                add_region(k, part, sets, [land], half, (dim,))
             else:
                 go(view(acc[k], k, part, sets, half), here, *sems, target)
 
@@ -607,14 +616,6 @@
         if arriving:
             add_region(k, part, mine, sources, None, gone)
 
-    pairs = [(k, part) for k in (1, 2, 0) for part in range(3)]
-    for k, part in pairs:
-        meet(k, part, 0)
-        ring(k, part, 1, False)
-    tok_cross()
-    v_c[c] = gv[...]
-    vec_start(0)
-
     def vec_next(n):
         total = vec_finish(n)
         if n < 3:
@@ -623,27 +624,157 @@
         else:
             out_v[...] = total
 
-    for k, part in pairs:
+    low = lanes_low(TILE)
+    scale = HEAD_DIM ** -0.5 * LOG2E
+    picker = (
+        lax.broadcasted_iota(jnp.int32, (8, 128), 0) == lax.broadcasted_iota(jnp.int32, (8, 128), 1) // HEAD_DIM
+    ).astype(jnp.float32)
+
+    def heads_back(pair, i):
+        cols = slice(pair * 128, (pair + 1) * 128)
+        qs, d_out = q_ref[i, :, cols], do_ref[i, :, cols]
+        none = jnp.zeros_like(qs)
+        q_heads = (jnp.where(low, qs, none), jnp.where(low, none, qs))
+        do_heads = (jnp.where(low, d_out, none), jnp.where(low, none, d_out))
+        prod = d_out.astype(jnp.float32) * o_ref[i, :, cols].astype(jnp.float32)
+        deltas = lax.dot_general(
+            picker, prod, (((1,), (1,)), ((), ())), precision=lax.Precision.HIGHEST, preferred_element_type=jnp.float32
+        )
+        if i == 0:
+            dkv[...] = jnp.zeros_like(dkv)
+        dq_acc[...] = jnp.zeros_like(dq_acc)
+
+        def step(n, carry):
+            t = q + 2 * i + n
+            k, v = kv[0, t, :, cols], kv[1, t, :, cols]
+            k_flip = flipped(k)
+            same = q_docs[i] == k_docs[t]
+            dk, dv = [], []
+            for head in range(2):
+                lanes = slice(head * HEAD_DIM, (head + 1) * HEAD_DIM)
+                scores = across_lanes(k, q_heads[head]) * scale
+                p = jnp.where(same, jnp.exp2(scores - lse_ref[pair, i, head : head + 1]), 0.0)
+                dp = across_lanes(v, do_heads[head])
+                ds = (p * (dp - deltas[head : head + 1])).astype(jnp.bfloat16)
+                dq_acc[lanes] += dot32(k_flip[lanes], ds)
+                dk.append(dot32(ds, q_heads[head]))
+                dv.append(dot32(p.astype(jnp.bfloat16), do_heads[head]))
+            dkv[0, t] += dk[0] + dk[1]
+            dkv[1, t] += dv[0] + dv[1]
+            return carry
+
+        lax.fori_loop(0, 9, step, 0)
+        dq_all[i, :, cols] = flipped(dq_acc[...] * HEAD_DIM ** -0.5).astype(jnp.bfloat16)
+        if i == 1:
+            def keep(t, carry):
+                dkv_all[0, t, :, cols] = (dkv[0, t] * HEAD_DIM ** -0.5).astype(jnp.bfloat16)
+                dkv_all[1, t, :, cols] = dkv[1, t].astype(jnp.bfloat16)
+                return carry
+
+            lax.fori_loop(0, 12, keep, 0)
+
+    def tile_back(group, n):
+        core, h = n // 2, lax.rem(n, 2)
+        t = group * 4 + n
+        x_flip = flipped(window[t])
+        dk, dv = dkv_all[0, t], dkv_all[1, t]
+        dw[1] += dot32(x_flip, dk)
+        dw[2] += dot32(x_flip, dv)
+        v_rows[...] = v_rows[...] + jnp.sum(dv.astype(jnp.float32), axis=0, keepdims=True)
+        dx = across_lanes(dk, w_heads[1]) + across_lanes(dv, w_heads[2])
+        t_all[core, group, h] = dx.astype(jnp.bfloat16)
+        if group == 1:
+            @pl.when(h == q)
+            def _():
+                dq = dq_all[core]
+                dw[0] += dot32(x_flip, dq)
+                q_rows[...] = q_rows[...] + jnp.sum(dq.astype(jnp.float32), axis=0, keepdims=True)
+                t_all[core, group, h] = (dx + across_lanes(dq, w_heads[0])).astype(jnp.bfloat16)
+
+    def tiles_back(group):
+        lax.fori_loop(0, 4, lambda n, carry: (tile_back(group, n), carry)[1], 0)
+
+    parts = range(3)
+    late = [(k, part) for k in (1, 2) for part in parts]
+    for k, part in late:
+        meet(k, part, 0)
+        ring(k, part, 1, False)
+    loads[0].wait()
+    heads_back(0, 0)
+    for k, part in late:
         meet(k, part, 1)
         meet(k, part, 2)
-        ring(k, part, 1, True)
-        ring(k, part, 2, False)
+    for part in parts:
+        ring(1, part, 1, True)
+        ring(1, part, 2, False)
+    heads_back(0, 1)
+    for part in parts:
+        ring(2, part, 1, True)
+        ring(2, part, 2, False)
+    heads_back(1, 0)
+    for k, part in late:
+        meet(k, part, 3)
+    meet_out()
+    heads_back(1, 1)
+    for part in parts:
+        ring(1, part, 2, True)
+        near(1, part, 1, False)
+    heads_back(2, 0)
+    for part in parts:
+        ring(2, part, 2, True)
+        near(2, part, 1, False)
+    for part in parts:
+        near(1, part, 1, True)
+        near(1, part, 2, False)
+    heads_back(2, 1)
+    for part in parts:
+        near(2, part, 1, True)
+        near(2, part, 2, False)
+    loads[1].wait()
+    loads[2].wait()
+    dw[...] = jnp.zeros_like(dw)
+    q_rows[...] = jnp.zeros_like(q_rows)
+    v_rows[...] = jnp.zeros_like(v_rows)
+    tiles_back(0)
+    tok_twin(0, 0)
+    tiles_back(2)
+    tok_twin(2, 6)
+    for k, part in late:
+        near(k, part, 2, True)
+    tiles_back(1)
+    tok_twin(1, 7)
+
+    def grads_low(i, carry):
+        rows_at = pl.ds(pl.multiple_of(i * 192, 192), 192)
+        for number, (a, b) in enumerate(((0, 0), (0, 1), (1, 0))):
+            acc[0][a, b, i] = dw[number, rows_at].reshape(4, 2, 3, 8, HALF).astype(jnp.bfloat16)
+        return carry
+
+    lax.fori_loop(0, 4, grads_low, 0)
+    for part in parts:
+        ring(0, part, 1, False)
+    v_c[c] = gv[...]
+    half_cols = pl.ds(pl.multiple_of(c * HALF, 128), HALF)
+    v_c[c, 0:1, half_cols] = q_rows[...]
+    v_c[c, 1:2, half_cols] = v_rows[...]
+    vec_start(0)
+    tok_edges()
     vec_next(0)
-    for k, part in pairs:
-        meet(k, part, 3)
+    for part in parts:
+        ring(0, part, 1, True)
+        ring(0, part, 2, False)
     vec_next(1)
+    for part in parts:
+        ring(0, part, 2, True)
+        near(0, part, 1, False)
+    vec_next(2)
+    for part in parts:
+        near(0, part, 1, True)
+        near(0, part, 2, False)
     tok_theirs()
-    vec_next(2)
-    for k, part in pairs:
-        ring(k, part, 2, True)
-        near(k, part, 1, False)
     vec_next(3)
-    tok_done = tok_mine()
-    for k, part in pairs:
-        near(k, part, 1, True)
-        near(k, part, 2, False)
-    for k, part in pairs:
-        near(k, part, 2, True)
+    for part in parts:
+        near(0, part, 2, True)
 
     for k in range(2):
         for part in range(3):
@@ -703,14 +834,14 @@
         t_twin.wait_send()
         t_cross.wait_send()
 
+    tok_mine().wait()
     for cp in kept:
         cp.wait()
-    tok_done.wait()
     for cp in sent:
         cp.wait_send()
 
 
-def reduce_all(g0, g0_other, g1, g2, gv, dx, base):
+def back(q_docs, k_docs, q_heads, d_heads, o_heads, lse, gv, kv, window, first, dwo, g1, g2, base):
     bf, f32, dma = jnp.bfloat16, jnp.float32, pltpu.SemaphoreType.DMA
     lands = []
     for part in range(3):
@@ -718,15 +849,15 @@
         for phase in range(3):
             size = dict(DIM_SIZE)
             for dim, names in (("x", ("x",)), ("y", ("m", "yp")), ("z", ("zh", "q"))):
-                if phase > 0 and dim in order[: phase + 1]:
+                if dim in order[: phase + 1]:
                     for name in names:
                         size[name] = 1
-            count = 2 if phase == 0 else EXTENT[order[phase]] - 1
-            lands += [pltpu.VMEM((count, *(size[d] for d in dims_of(k)), 8, HALF), bf) for k in STREAMS]
+            count = (2, 2) if phase == 0 else (EXTENT[order[phase]] - 1,)
+            lands += [pltpu.VMEM((*count, *(size[d] for d in dims_of(k)), 8, HALF), bf) for k in STREAMS]
     whole = [pltpu.VMEM(WIDE, bf), pltpu.VMEM(TALL, bf)]
     return pl.pallas_call(
-        reduce_kernel,
-        name="reduce_all",
+        back_kernel,
+        name="back",
         out_shape=(
             jax.ShapeDtypeStruct((6, 3072), f32),
             jax.ShapeDtypeStruct((6, 3072), f32),
@@ -734,7 +865,7 @@
             jax.ShapeDtypeStruct((16, 768), f32),
             jax.ShapeDtypeStruct((TILE, 768), f32),
         ),
-        in_specs=[ANY_SPACE, ANY_SPACE, ANY_SPACE, ANY_SPACE, IN_VMEM, ANY_SPACE, ANY_SPACE],
+        in_specs=[IN_VMEM] * 7 + [ANY_SPACE] * 7,
         out_specs=(ANY_SPACE, ANY_SPACE, ANY_SPACE, IN_VMEM, ANY_SPACE),
         scratch_shapes=[
             pltpu.VMEM(WIDE, bf), *whole, pltpu.VMEM((4, 4, 2, 3, 8, HALF), bf), *whole, *lands,
@@ -745,19 +876,28 @@
             pltpu.VMEM((4, 16, 768), f32),
             pltpu.VMEM((4, 16, 768), f32),
             pltpu.VMEM((8, 16, 768), f32),
-            pltpu.VMEM((3, 2, TILE, 768), bf),
+            pltpu.VMEM((2, 3, 2, TILE, 768), bf),
             pltpu.VMEM((3, 2, TILE, 768), bf),
             pltpu.VMEM((2, 2, TILE, 768), bf),
             pltpu.VMEM((TILE, 768), bf),
             pltpu.VMEM((TILE, 768), bf),
             pltpu.VMEM((TILE, 768), f32),
-            pltpu.VMEM((TILE, 768), f32),
+            pltpu.VMEM((2, 12, TILE, HALF), bf),
+            pltpu.VMEM((12, TILE, 768), bf),
+            pltpu.VMEM((3, 768, HALF), bf),
+            pltpu.VMEM((2, 12, TILE, HALF), bf),
+            pltpu.VMEM((2, 12, TILE, 128), f32),
+            pltpu.VMEM((2, TILE, HALF), bf),
+            pltpu.VMEM((128, TILE), f32),
+            pltpu.VMEM((3, 768, HALF), f32),
+            pltpu.VMEM((1, HALF), f32),
+            pltpu.VMEM((1, HALF), f32),
             dma((12, 3)), dma((12, 3)), dma((12, 3)), dma((3, 2, 8, 3)), dma((3, 2, 8, 3)), dma((6, 2, 3)), dma((6, 2, 3)),
             dma((2, 8)), dma((2, 7)),
-            dma((2,)), dma((3,)), dma((4, 8)), dma((4, 8)), dma((6,)), dma((6,)), dma((3,)),
+            dma((2,)), dma((3,)), dma((4, 8)), dma((4, 8)), dma((8,)), dma((8,)), dma((1,)), dma((5,)),
         ],
-        compiler_params=pltpu.CompilerParams(collective_id=2, has_side_effects=True, vmem_limit_bytes=60 << 20),
-    )(g0, g0_other, g1, g2, gv, dx, base)
+        compiler_params=pltpu.CompilerParams(collective_id=2, has_side_effects=True, vmem_limit_bytes=63 << 20),
+    )(q_docs, k_docs, q_heads, d_heads, o_heads, lse, gv, kv, window, first, dwo, g1, g2, base)
 
 
 def to_tokens_kernel(heads, rows, send, recv, local):
@@ -826,10 +966,8 @@
         def _():
             q_ref[i] = (dot32(x, w_ref[0, 0]) + bq_ref[0]).astype(jnp.bfloat16)
 
-    @pl.when(jnp.logical_and(t >= plan[7], t < plan[8]))
-    def _():
-        kv_ref[0, 0] = dot32(x, w_ref[0, 1]).astype(jnp.bfloat16)
-        kv_ref[1, 0] = (dot32(x, w_ref[0, 2]) + bv_ref[0]).astype(jnp.bfloat16)
+    kv_ref[0, 0] = dot32(x, w_ref[0, 1]).astype(jnp.bfloat16)
+    kv_ref[1, 0] = (dot32(x, w_ref[0, 2]) + bv_ref[0]).astype(jnp.bfloat16)
 
 
 def project(plan, window, first, bias_q, bias_v):
@@ -923,146 +1061,6 @@
         ),
         compiler_params=pltpu.CompilerParams(vmem_limit_bytes=58 << 20),
     )(plan, q_docs, k_docs, q_heads, kv)
-
-
-def attend_back_kernel(plan, q_docs, k_docs, q_ref, do_ref, o_ref, lse_ref, kv, dq_ref, dkv_ref, dkv, dq):
-    i = pl.program_id(1)
-    low = lanes_low(TILE)
-
-    @pl.when(i == 0)
-    def _():
-        dkv[...] = jnp.zeros_like(dkv)
-
-    q, d_out = q_ref[0], do_ref[0]
-    none = jnp.zeros_like(q)
-    q_heads = (jnp.where(low, q, none), jnp.where(low, none, q))
-    do_heads = (jnp.where(low, d_out, none), jnp.where(low, none, d_out))
-    prod = d_out.astype(jnp.float32) * o_ref[0].astype(jnp.float32)
-    first = lax.broadcasted_iota(jnp.int32, (8, 128), 0)
-    halves = lax.broadcasted_iota(jnp.int32, (8, 128), 1) // HEAD_DIM
-    deltas = lax.dot_general(
-        (first == halves).astype(jnp.float32), prod, (((1,), (1,)), ((), ())),
-        precision=lax.Precision.HIGHEST, preferred_element_type=jnp.float32,
-    )
-    deltas = (deltas[0:1], deltas[1:2])
-    lses = (lse_ref[0, 0, 0:1], lse_ref[0, 0, 1:2])
-    docs = q_docs[0]
-    dq[...] = jnp.zeros_like(dq)
-    scale = HEAD_DIM ** -0.5 * LOG2E
-
-    def step(j, carry):
-        k, v = kv[0, j], kv[1, j]
-        k_flip = flipped(k)
-        same = docs == k_docs[j]
-        dk, dv = [], []
-        for head in range(2):
-            rows = slice(head * HEAD_DIM, (head + 1) * HEAD_DIM)
-            s = across_lanes(k, q_heads[head]) * scale
-            p = jnp.where(same, jnp.exp2(s - lses[head]), 0.0)
-            dp = across_lanes(v, do_heads[head])
-            ds = (p * (dp - deltas[head])).astype(jnp.bfloat16)
-            dq[rows] += dot32(k_flip[rows], ds)
-            dk.append(dot32(ds, q_heads[head]))
-            dv.append(dot32(p.astype(jnp.bfloat16), do_heads[head]))
-        dkv[0, j] += dk[0] + dk[1]
-        dkv[1, j] += dv[0] + dv[1]
-        return carry
-
-    lax.fori_loop(plan[3 + 2 * i], plan[4 + 2 * i], step, 0)
-    dq_ref[0] = flipped(dq[...] * HEAD_DIM ** -0.5).astype(jnp.bfloat16)
-
-    @pl.when(i == 1)
-    def _():
-        dkv_ref[0] = (dkv[0] * HEAD_DIM ** -0.5).astype(jnp.bfloat16)
-        dkv_ref[1] = dkv[1].astype(jnp.bfloat16)
-
-
-def attend_back(plan, q_docs, k_docs, q_heads, d_heads, o_heads, lse, kv):
-    return pl.pallas_call(
-        attend_back_kernel,
-        name="attend_back",
-        grid_spec=pltpu.PrefetchScalarGridSpec(
-            num_scalar_prefetch=1,
-            grid=(3, 2),
-            in_specs=[*DOC_SPECS, OWN_PAIR, OWN_PAIR, OWN_PAIR, STATS, WINDOW_PAIR],
-            out_specs=[OWN_PAIR, WINDOW_PAIR],
-            scratch_shapes=[
-                pltpu.VMEM((2, 12, TILE, 128), jnp.float32),
-                pltpu.VMEM((128, TILE), jnp.float32),
-            ],
-        ),
-        out_shape=(
-            jax.ShapeDtypeStruct((2, TILE, HALF), jnp.bfloat16),
-            jax.ShapeDtypeStruct((2, 12, TILE, HALF), jnp.bfloat16),
-        ),
-        compiler_params=pltpu.CompilerParams(vmem_limit_bytes=58 << 20),
-    )(plan, q_docs, k_docs, q_heads, d_heads, o_heads, lse, kv)
-
-
-def project_back_kernel(plan, x_ref, w_ref, dq_ref, dkv_ref, dw_ref, dx_ref, sums_ref, dw, sums):
-    t = pl.program_id(0)
-
-    @pl.when(t == 0)
-    def _():
-        dw[...] = jnp.zeros_like(dw)
-        sums[...] = jnp.zeros_like(sums)
-
-    used = jnp.logical_and(t >= plan[7], t < plan[8])
-
-    @pl.when(used)
-    def _():
-        x_flip = flipped(x_ref[0])
-        dk, dv = dkv_ref[0, 0], dkv_ref[1, 0]
-        dw[1] += dot32(x_flip, dk)
-        dw[2] += dot32(x_flip, dv)
-        sums[1:2] += jnp.sum(dv.astype(jnp.float32), axis=0, keepdims=True)
-        dx = across_lanes(dk, w_ref[0, 1]) + across_lanes(dv, w_ref[0, 2])
-        dx_ref[0] = dx.astype(jnp.bfloat16)
-        for i in range(2):
-            @pl.when(t == plan[1 + i])
-            def _():
-                dq = dq_ref[i]
-                dw[0] += dot32(x_flip, dq)
-                sums[0:1] += jnp.sum(dq.astype(jnp.float32), axis=0, keepdims=True)
-                dx_ref[0] = (dx + across_lanes(dq, w_ref[0, 0])).astype(jnp.bfloat16)
-
-    @pl.when(jnp.logical_not(used))
-    def _():
-        dx_ref[...] = jnp.zeros_like(dx_ref)
-
-    @pl.when(t == 11)
-    def _():
-        dw_ref[...] = dw[...].astype(jnp.bfloat16)
-        sums_ref[...] = sums[...]
-
-
-def project_back(plan, window, first, dq, dkv):
-    return pl.pallas_call(
-        project_back_kernel,
-        name="project_back",
-        grid_spec=pltpu.PrefetchScalarGridSpec(
-            num_scalar_prefetch=1,
-            grid=(12,),
-            in_specs=[
-                pl.BlockSpec((1, TILE, 768), lambda t, p: (t, 0, 0)),
-                pl.BlockSpec((1, 4, 768, HALF), lambda t, p: (p[0], 0, 0, 0)),
-                pl.BlockSpec((2, TILE, HALF), lambda t, p: (0, 0, 0)),
-                pl.BlockSpec((2, 1, TILE, HALF), lambda t, p: (0, t, 0, 0)),
-            ],
-            out_specs=[
-                pl.BlockSpec((3, 768, HALF), lambda t, p: (0, 0, 0)),
-                pl.BlockSpec((1, TILE, 768), lambda t, p: (t, 0, 0)),
-                pl.BlockSpec((8, HALF), lambda t, p: (0, 0)),
-            ],
-            scratch_shapes=[pltpu.VMEM((3, 768, HALF), jnp.float32), pltpu.VMEM((8, HALF), jnp.float32)],
-        ),
-        out_shape=(
-            jax.ShapeDtypeStruct((3, 768, HALF), jnp.bfloat16),
-            jax.ShapeDtypeStruct((12, TILE, 768), jnp.bfloat16),
-            jax.ShapeDtypeStruct((8, HALF), jnp.float32),
-        ),
-        compiler_params=pltpu.CompilerParams(vmem_limit_bytes=58 << 20),
-    )(plan, window, first, dq, dkv)
 
 
 def norm_parts(resid):
@@ -1241,18 +1239,10 @@
         attended, tokens, cotangent, rows, hidden_bias, first, second, third
     )
     d_heads = swap(to_heads_kernel, "to_heads", (2, TILE, HALF), 5, d_att)
-    dq, dkv = attend_back(plan, query_docs, key_docs, q_heads, d_heads, o_heads, lse, kv)
-    dw_qkv, dx, head_sums = project_back(plan, window, first, dq, dkv)
-
-    mine = jnp.arange(2) == core
-    dw_out_mine = lax.dynamic_index_in_dim(dw_out, core, 0)
-    dw_out_other = lax.dynamic_index_in_dim(dw_out, 1 - core, 0, keepdims=False)
-    grad_first = jnp.concatenate([dw_qkv, dw_out_mine], axis=0)
-    both = jnp.where(mine[None, :, None], head_sums[:2, None], 0.0).reshape(2, width)
-    vec_sums = jnp.concatenate([both, sums[2:], sums_in.reshape(4, width), jnp.zeros((4, width), f32)], axis=0)
-    sum_first, sum_in, sum_down, sum_vec, grad_tokens = reduce_all(
-        grad_first.reshape(WIDE), dw_out_other.reshape(4, 4, 2, 3, 8, HALF), dw_in.reshape(2, *WIDE), dw_down.reshape(2, *TALL), vec_sums,
-        dx.reshape(3, 2, 2, TILE, width), d_one,
+    vec_sums = jnp.concatenate([sums, sums_in.reshape(4, width), jnp.zeros((4, width), f32)], axis=0)
+    sum_first, sum_in, sum_down, sum_vec, grad_tokens = back(
+        query_docs, key_docs, q_heads, d_heads, o_heads, lse, vec_sums, kv, window, first,
+        dw_out.reshape(2, 4, 4, 2, 3, 8, HALF), dw_in.reshape(2, *WIDE), dw_down.reshape(2, *TALL), d_one,
     )
     own = lax.dynamic_slice(sum_vec, (0, 6 * shard), (8, 6))
     own_in = lax.dynamic_slice(sum_vec[8:12].reshape(-1), (24 * shard,), (24,))

time: 391 us -> 345 us (0.88)
  the two profiles are of different devices: /device:TPU:55 before, /device:TPU:1 now
where the time goes in v1:
time: 345 us; the launch traced here: 340 us
  Pallas kernels  306 us (89%)
  local copies, waits for them, and re-layouts  23.5 us (7%)
  other arithmetic  10.2 us (3%)
    pallas_call x1, Pallas kernels, back(): pl.pallas_call(back_kernel, name='back', out_shape=(jax.ShapeDtypeStruct(...  147 us
    pallas_call x1, Pallas kernels, gather(): pl.pallas_call(gather_kernel, name='gather', out_shape=(jax.ShapeDtypeStr...  87.7 us
    pallas_call x1, Pallas kernels, mlp(): pl.pallas_call(mlp_kernel, name='mlp', in_specs=[IN_VMEM] * 5 + [ANY_SPAC...  27.4 us
    pallas_call x1, Pallas kernels, attend(): pl.pallas_call(attend_kernel, name='attend', grid_spec=pltpu.PrefetchScal...  25 us
    pallas_call x1, Pallas kernels, project(): pl.pallas_call(project_kernel, name='project', grid_spec=pltpu.PrefetchSc...  14 us

profile of v1, /device:TPU:1, one launch (start us, length us, event | category | flops | bytes accessed | tf_op | source)
XLA Modules:
  0.0 340.3 jit_solution(7269010798071273732)
XLA Ops:
  0.7 0.8 copy.39
  1.7 0.7 sub.20
  2.4 1.8 convert_reduce_fusion
  6.1 4.5 %stack.51.plan = s32[9]{0:T(128)} concatenate(s32[1]{0:T(128)} %bitcast, s32[1]{0:T(128)} %bitcast.1, s32[1]{0:T(128)} %bitcast.2, s32[1]{0:T(128)} %get-tuple-element.76, s32[1]{0:T(128)} %get-tuple-element.74, s32[1]{0:T(128)} %get-tuple-element.75, s32[1]{0:T(128)} %get-tuple-element.73, s32[1]{0:T(128)} %get-tuple-element.76, s32[1]{0:T(128)} %get-tuple-element.73), dimensions={0} | concatenate | bytes 72 | tf_op jit(solution)/shard_map/stack | solution.py:1213
  10.6 0.8 maximum_bitcast_fusion
  11.4 1.5 pad_maximum_fusion.cat_ref
  12.8 0.8 stack.63
  13.6 0.7 pad_convert_fusion
  14.4 0.7 maximum_maximum_fusion.1.vec_ref
  15.0 87.7 %gather.1 = (bf16[2,2,2,4,4,2,3,8,384]{8,7,6,5,4,3,2,1,0:T(8,128)(2,1)}, bf16[2,2,2,4,4,2,3,8,384]{8,7,6,5,4,3,2,1,0:T(8,128)(2,1)}, bf16[2,4,4,2,2,2,3,8,384]{8...) custom-call(bf16[2,6,3072]{2,1,0:T(8,128)(2,1)} %pad_maximum_fusion.cat_ref, ...), custom_call_target="tpu_custom_call" | custom-call | tf_op jit(solution)/shard_map/gather/pallas_call | solution.py:356
  102.8 1.1 copy.41
  104.2 0.7 reshape_squeeze.12.bq_ref
  104.9 0.7 reshape_squeeze.13.bv_ref
  105.7 14.0 %project.1 = (bf16[2,256,384]{2,1,0:T(8,128)(2,1)}, bf16[2,12,256,384]{3,2,1,0:T(8,128)(2,1)}) custom-call(s32[9]{0:T(128)} %stack.51.plan, bf16[12,256,768]{2,1,0:T(8,128)(2,1)} %bitcast.47, bf16[2,4,768,384]{3,2,1,0:T(8,128)(2,1)} %bitcast.44, f32[2,1,384]{2,1,0:T(1,128)} %reshape_squeeze.12.bq_ref, f32[2,1,384]{2,1,0:T(1,128)} %reshape_squeeze.13.bv_ref), custom_call_target="tpu_custom_call" | custom-call | tf_op jit(solution)/shard_map/project/pallas_call | solution.py:975
  119.7 1.4 sub.24
  121.1 1.4 fusion.k_docs.refs_1_
  123.1 25.0 %attend.1 = (bf16[2,256,384]{2,1,0:T(8,128)(2,1)}, f32[3,2,2,256]{3,2,1,0:T(2,128)}) custom-call(s32[9]{0:T(128)} %stack.51.plan, s32[2,1,256]{2,1,0:T(1,128)} %reshape.154.q_docs.refs_0_, s32[12,256,1]{2,1,0:T(8,128)} %fusion.k_docs.refs_1_, bf16[2,256,384]{2,1,0:T(8,128)(2,1)} %get-tuple-element.40.q_ref.refs_2_, ...), custom_call_target="tpu_custom_call" | custom-call | tf_op jit(solution)/shard_map/attend/pallas_call | solution.py:1044
  148.1 2.4 to_tokens.1.att_ref
  150.6 0.9 reshape.160.rows
  151.7 0.7 reshape_squeeze.14.bias_in
  152.4 27.4 %mlp.1 = (bf16[256,768]{1,0:T(8,128)(2,1)}, f32[256,768]{1,0:T(8,128)}, bf16[256,768]{1,0:T(8,128)(2,1)}, bf16[2,768,384]{2,1,0:T(8,128)(2,1)}, bf16[2,4,768,384...) custom-call(bf16[256,768]{1,0:T(8,128)(2,1)} %to_tokens.1.att_ref, ...), custom_call_target="tpu_custom_call" | custom-call | tf_op jit(solution)/shard_map/mlp/pallas_call | solution.py:1165
  179.9 0.7 reduce.8
  180.7 1.4 maximum_maximum_fusion.refs_6_
  182.1 2.4 to_heads.1.refs_3_
  184.6 146.8 %back.1 = (f32[6,3072]{1,0:T(8,128)}, f32[6,3072]{1,0:T(8,128)}, f32[3,8,768]{2,1,0:T(8,128)}, f32[16,768]{1,0:T(8,128)}, f32[256,768]{1,0:T(8,128)}) custom-call(s32[2,1,256]{2,1,0:T(1,128)} %reshape.154.q_docs.refs_0_, s32[12,256,1]{2,1,0:T(8,128)} %fusion.k_docs.refs_1_, bf16[2,256,384]{2,1,0:T(8,128)(2,1)} %get-tuple-element.40.q_ref.refs_2_, ...), custom_call_target="tpu_custom_call" | custom-call | tf_op jit(solution)/shard_map/back/pallas_call | solution.py:858
  331.3 1.6 slice.91
  332.9 0.7 slice.98
  334.2 1.3 slice.94
  335.6 0.8 constant_dynamic-slice_fusion
  336.9 2.1 copy.49
  339.0 0.6 copy.50
  339.6 0.6 copy.51
  (30 shorter events, 4.7 us)
Async XLA Ops:
  331.3 7.6 %copy-start = (f32[6,3072]{1,0:T(8,128)S(1)}, f32[6,3072]{1,0:T(8,128)}, u32[]{:S(2)}) copy-start(f32[6,3072]{1,0:T(8,128)} %get-tuple-element.103) | copy-start | bytes 221188
  331.3 8.3 %copy-start.1 = (f32[3,8,768]{2,1,0:T(8,128)S(1)}, f32[3,8,768]{2,1,0:T(8,128)}, u32[]{:S(2)}) copy-start(f32[3,8,768]{2,1,0:T(8,128)} %get-tuple-element.58) | copy-start | bytes 221188
